TPU v7x, 512 devices: a whole 4x8x8 slice. The times are simulated.
512 devices in a mesh: tiles: 128 (over x, y_lo, z, core), bins: 4 (over y_hi).
Axes of the slice: x: 4, y: 8 (y_hi: 4, y_lo: 2; y = y_hi * 2 + y_lo), z: 8, core: 2. Of those that a mesh axis runs over, the one named last changes fastest.
Arguments:
- dust_state: float32 [4, 112, 512, 256], P(None, 'bins', 'tiles'), may hold values from -4 to 4, as said below
- drift_speed: float32 [112], P('bins'), may hold values from -0.5 to 0.5
- stop_ratio: float32 [112], P('bins'), may hold values from 0.05 to 20
- gas_rho: float32 [512, 256], P('tiles'), may hold values from 0.5 to 2
- gas_vel: float32 [3, 512, 256], P(None, 'tiles'), may hold values from -3 to 3
- pressure: float32 [512, 256], P('tiles'), may hold values from 0.5 to 2
- pair_list: int32 [6328, 2], replicated, may hold values from 0 to 111, as said below
- outcome: float32 [6328, 112], P(None, 'bins'), may hold values from -0.078125 to 0.078125
Outputs:
- dust_next: float32 [4, 112, 512, 256], P(None, 'bins', 'tiles')
Inputs may be any that keep to these rules, and one draw needn't show every extreme that they name: `dust_state`: field 0 lies in 0.3 to 3. `pair_list`: each unordered pair of bins, a bin with itself included, stands once, smaller bin first.
All inputs are finite; a program needn't handle non-finite values.
Results may differ from a plain program's by a relative error of at most 0.000065.
Values sent between devices are 32-bit elements; how exact they have to be, the bound alone decides.
A program may use at most 64 MiB of HBM per device.

v0:
```python
import jax
import jax.numpy as jnp
from jax import lax
from jax.sharding import PartitionSpec as P

coag_step = 0.5
pressure_coupling = 1.0


def from_everyone(value, axis):
    copies = jnp.broadcast_to(value, (lax.axis_size(axis), *value.shape))
    return lax.all_to_all(copies, axis, split_axis=0, concat_axis=0, tiled=True)


def in_order(blocks, dim):
    blocks = jnp.moveaxis(blocks, 0, dim)
    shape = blocks.shape
    return blocks.reshape(*shape[:dim], shape[dim] * shape[dim + 1], *shape[dim + 2 :])


def collect(value, axis, dim):
    blocks = from_everyone(value, axis)
    return in_order(blocks, dim)


def padded_2(value, sides, width):
    for axis, dim in sides:
        size, length = (lax.axis_size(axis), value.shape[dim])
        up = [(i, (i + 1) % size) for i in range(size - 1)]
        down = [(j, i) for i, j in up]
        last = lax.slice_in_dim(value, length - width, length, axis=dim)
        first = lax.slice_in_dim(value, 0, width, axis=dim)
        before = lax.ppermute(last, axis, up)
        after = lax.ppermute(first, axis, down)
        value = jnp.concatenate([before, value, after], axis=dim)
    return value


def flux_rate(padded, courant):
    upwind_pos = jnp.maximum(courant, 0.0)[None, :, None, None]
    upwind_neg = jnp.minimum(courant, 0.0)[None, :, None, None]
    minus_two = padded[:, :, :-4]
    minus_one = padded[:, :, 1:-3]
    centre = padded[:, :, 2:-2]
    plus_one = padded[:, :, 3:-1]
    plus_two = padded[:, :, 4:]
    face_upper = upwind_pos * (1.5 * centre - 0.5 * minus_one) + upwind_neg * (
        1.5 * plus_one - 0.5 * plus_two
    )
    face_lower = upwind_pos * (1.5 * minus_one - 0.5 * minus_two) + upwind_neg * (
        1.5 * centre - 0.5 * plus_one
    )
    return face_lower - face_upper


def coagulate(density, pair_list, outcome):
    whole = collect(density, "bins", 0)
    bin_count = whole.shape[0]
    bin_iota = jnp.arange(bin_count, dtype=jnp.int32)[None, :]
    first_hot = (pair_list[:, 0:1] == bin_iota).astype(jnp.float32)
    second_hot = (pair_list[:, 1:2] == bin_iota).astype(jnp.float32)
    blocks = whole.transpose(1, 0, 2)

    def one_block(piece):
        first_bins = jnp.dot(
            first_hot, piece, precision=lax.Precision.HIGHEST, preferred_element_type=jnp.float32
        )
        second_bins = jnp.dot(
            second_hot, piece, precision=lax.Precision.HIGHEST, preferred_element_type=jnp.float32
        )
        return lax.dot_general(
            outcome,
            first_bins * second_bins,
            (((0,), (0,)), ((), ())),
            precision=lax.Precision.HIGHEST,
            preferred_element_type=jnp.float32,
        )

    gained = lax.map(one_block, blocks)
    return gained.transpose(1, 0, 2)


def local(dust_state, drift_speed, stop_ratio, gas_rho, gas_vel, pressure, pair_list, outcome):
    rows_here = dust_state.shape[2]
    widened = padded_2(dust_state, (("tiles", 2),), 4)
    section_wide = widened[:, :, 2:-2] + flux_rate(widened, drift_speed)
    position = lax.axis_index("tiles") * rows_here - 2 + jnp.arange(rows_here + 4, dtype=jnp.int32)
    inside = (position >= 0) & (position < rows_here * lax.axis_size("tiles"))
    section_wide = jnp.where(inside[None, None, :, None], section_wide, 0.0)
    moved = 0.5 * (dust_state + section_wide[:, :, 2:-2] + flux_rate(section_wide, drift_speed))
    source = coagulate(moved[0], pair_list, outcome)
    density = moved[0] + coag_step * source
    grown = moved[1:] + coag_step * source[None] * gas_vel[:, None]
    padded_pressure = padded_2(pressure, (("tiles", 0),), 1)
    gradient = (padded_pressure[2:] - padded_pressure[:-2]) / (2.0 * gas_rho)
    target = jnp.concatenate([(gas_vel[0] - pressure_coupling * gradient)[None], gas_vel[1:]], 0)
    coupling = stop_ratio[None, :, None, None]
    momenta = (grown + coupling * density[None] * target[:, None]) / (1.0 + coupling)
    return jnp.concatenate([density[None], momenta], 0)


def solution(mesh):
    return jax.shard_map(
        local,
        mesh=mesh,
        in_specs=(
            P(None, "bins", "tiles", None),
            P("bins"),
            P("bins"),
            P("tiles", None),
            P(None, "tiles", None),
            P("tiles", None),
            P(),
            P(None, "bins"),
        ),
        out_specs=P(None, "bins", "tiles", None),
        check_vma=False,
    )
```

profile of v0, /device:TPU:6, one launch (start us, length us, event | category | flops | bytes accessed | tf_op | source)
XLA Modules:
  0.0 128.6 jit_solution(12659498179086444850)
XLA Ops:
  0.0 2.0 %collective-permute-start = (f32[4,28,4,256]{3,2,1,0:T(4,128)}, f32[4,28,4,256]{3,2,1,0:T(4,128)S(1)}, u32[]{:S(2)}, u32[]{:S(2)}) collective-permute-start(f32[4,28,4,256]{3,2,1,0:T(4,128)} %param.10), channel_id=1, source_target_pairs={{0,4},{4,8},{8,12},{12,16},{16,20},{20,24},{24,28},{28,32},{32,36}... | collective-permute-start | bytes 1376264 | tf_op jit(solution)/shard_map/ppermute | solution.py:33
  2.1 11.7 %collective-permute-start.1 = (f32[4,28,4,256]{3,2,1,0:T(4,128)}, f32[4,28,4,256]{3,2,1,0:T(4,128)S(1)}, u32[]{:S(2)}, u32[]{:S(2)}) collective-permute-start(f32[4,28,4,256]{3,2,1,0:T(4,128)} %param.10), channel_id=1, source_target_pairs={{4,0},{8,4},{12,8},{16,12},{20,16},{24,20},{28,24},{32,28},{36,32}... | collective-permute-start | bytes 1376264 | tf_op jit(solution)/shard_map/ppermute | solution.py:34
  14.4 3.7 %collective-permute-done = f32[4,28,4,256]{3,2,1,0:T(4,128)S(1)} collective-permute-done((f32[4,28,4,256]{3,2,1,0:T(4,128)}, f32[4,28,4,256]{3,2,1,0:T(4,128)S(1)}, u32[]{:S(2)}, u32[]{:S(2)}) %collective-permute-start) | collective-permute-done | bytes 458784 | tf_op jit(solution)/shard_map/ppermute | solution.py:33
  18.2 1.9 %collective-permute-done.1 = f32[4,28,4,256]{3,2,1,0:T(4,128)S(1)} collective-permute-done((f32[4,28,4,256]{3,2,1,0:T(4,128)}, f32[4,28,4,256]{3,2,1,0:T(4,128)S(1)}, u32[]{:S(2)}, u32[]{:S(2)}) %collective-permute-start.1) | collective-permute-done | bytes 458784 | tf_op jit(solution)/shard_map/ppermute | solution.py:34
  20.0 1.3 %pad_maximum_fusion = f32[4,28,12,256]{3,2,1,0:T(8,128)S(1)} fusion(f32[4,28,4,256]{3,2,1,0:T(4,128)S(1)} %collective-permute-done.1, f32[4,28,4,256]{3,2,1,0:T(4,128)} %param.10, f32[4,28,4,256]{3,2,1,0:T(4,128)S(1)} %collective-permute-done), kind=kLoop, calls=%fused_computation.13 | loop fusion | flops 688128 | bytes 2752512 | tf_op jit(solution)/shard_map/concatenate | solution.py:35
  21.4 1.1 fusion.14
  24.3 6.2 %all-to-all-start = ((f32[4,28,4,256]{3,2,1,0:T(4,128)}), f32[4,28,4,256]{3,2,1,0:T(4,128)S(1)}, u32[]{:S(2)}, u32[]{:S(2)}) async-start(f32[4,28,4,256]{3,2,1,0:T(4,128)} %broadcast_in_dim.42), calls=%async_computation | async-start | bytes 917504 | tf_op jit(solution)/shard_map/all_to_all | solution.py:12
  30.5 6.4 %collective-permute-start.2 = (f32[1,256]{1,0:T(1,128)S(1)}, f32[1,256]{1,0:T(1,128)S(1)}, u32[]{:S(2)}, u32[]{:S(2)}) collective-permute-start(f32[1,256]{1,0:T(1,128)S(1)} %get-tuple-element.77), channel_id=1, source_target_pairs={{4,0},{8,4},{12,8},{16,12},{20,16},{24,20},{28,24},{32,28},{36,32}... | collective-permute-start | bytes 3080 | tf_op jit(solution)/shard_map/ppermute | solution.py:34
  36.9 1.9 %collective-permute-start.3 = (f32[1,256]{1,0:T(1,128)S(1)}, f32[1,256]{1,0:T(1,128)S(1)}, u32[]{:S(2)}, u32[]{:S(2)}) collective-permute-start(f32[1,256]{1,0:T(1,128)S(1)} %get-tuple-element.78), channel_id=1, source_target_pairs={{0,4},{4,8},{8,12},{12,16},{16,20},{20,24},{24,28},{28,32},{32,36}... | collective-permute-start | bytes 3080 | tf_op jit(solution)/shard_map/ppermute | solution.py:33
  39.1 5.8 %collective-permute-done.3 = f32[1,256]{1,0:T(1,128)S(1)} collective-permute-done((f32[1,256]{1,0:T(1,128)S(1)}, f32[1,256]{1,0:T(1,128)S(1)}, u32[]{:S(2)}, u32[]{:S(2)}) %collective-permute-start.3) | collective-permute-done | bytes 1056 | tf_op jit(solution)/shard_map/ppermute | solution.py:33
  44.9 82.5 %while.11 = (s32[]{:T(128)}, f32[4,28,256]{2,0,1:T(4,128)S(1)}, f32[4,112,256]{2,0,1:T(4,128)S(1)}, f32[6328,28]{0,1:T(8,128)S(1)}, s32[6328]{0:T(1024)S(1)}, /*index=5*/s32[6328]{0:T(1024)S(1)}, s32[]{:T(128)}, s32[]{:T(128)}) while((s32[]{:T(128)}, f32[4,28,256]{2,0,1:T(4,128)S(1)}, f32[4,112,256]{2,0,1:T(4,128)S(1)}, ...), condition=%wide.region_1.2_spmd.clone, body=%wide.region_0.1_spmd.clone.sunk | while | flops 4903238144 | bytes 27281052 | solution.py:79
  45.2 7.2 %fusion.45 = f32[256,6328]{1,0:T(8,128)S(1)} fusion(s32[6328]{0:T(1024)S(1)} %get-tuple-element.138, f32[1,112,256]{2,0,1:T(1,128)S(1)} %constant_dynamic-slice_fusion.2), kind=kOutput, calls=%fused_computation.5.clone.1 | convolution fusion | flops 2178654464 | bytes 6619872 | tf_op jit(solution)/shard_map/while/body/eval_jaxpr/dot_general | solution.py:65
  52.4 7.4 %convolution_multiply_fusion.2 = f32[256,6328]{1,0:T(8,128)S(1)} fusion(f32[256,6328]{1,0:T(8,128)S(1)} %fusion.45, s32[6328]{0:T(1024)S(1)} %get-tuple-element.139, f32[1,112,256]{2,0,1:T(1,128)S(1)} %constant_dynamic-slice_fusion.2), kind=kOutput, calls=%fused_computation.2.clone.1 | convolution fusion | flops 2180274432 | bytes 13099744 | tf_op jit(solution)/shard_map/while/body/eval_jaxpr/dot_general | solution.py:68
  59.8 5.7 %convolution_bitcast_fusion.2 = f32[1,28,256]{2,1,0:T(8,128)S(1)} fusion(f32[256,6328]{1,0:T(8,128)S(1)} %convolution_multiply_fusion.2, f32[6328,28]{0,1:T(8,128)S(1)} %get-tuple-element.137), kind=kOutput, calls=%fused_computation.10.clone.1 | convolution fusion | flops 544309248 | bytes 7217280 | tf_op jit(solution)/shard_map/while/body/eval_jaxpr/dot_general | solution.py:71
  65.8 7.2 %fusion.45 = f32[256,6328]{1,0:T(8,128)S(1)} fusion(s32[6328]{0:T(1024)S(1)} %get-tuple-element.138, f32[1,112,256]{2,0,1:T(1,128)S(1)} %constant_dynamic-slice_fusion.2), kind=kOutput, calls=%fused_computation.5.clone.1 | convolution fusion | flops 2178654464 | bytes 6619872 | tf_op jit(solution)/shard_map/while/body/eval_jaxpr/dot_general | solution.py:65
  73.0 7.4 %convolution_multiply_fusion.2 = f32[256,6328]{1,0:T(8,128)S(1)} fusion(f32[256,6328]{1,0:T(8,128)S(1)} %fusion.45, s32[6328]{0:T(1024)S(1)} %get-tuple-element.139, f32[1,112,256]{2,0,1:T(1,128)S(1)} %constant_dynamic-slice_fusion.2), kind=kOutput, calls=%fused_computation.2.clone.1 | convolution fusion | flops 2180274432 | bytes 13099744 | tf_op jit(solution)/shard_map/while/body/eval_jaxpr/dot_general | solution.py:68
  80.4 5.7 %convolution_bitcast_fusion.2 = f32[1,28,256]{2,1,0:T(8,128)S(1)} fusion(f32[256,6328]{1,0:T(8,128)S(1)} %convolution_multiply_fusion.2, f32[6328,28]{0,1:T(8,128)S(1)} %get-tuple-element.137), kind=kOutput, calls=%fused_computation.10.clone.1 | convolution fusion | flops 544309248 | bytes 7217280 | tf_op jit(solution)/shard_map/while/body/eval_jaxpr/dot_general | solution.py:71
  86.4 7.2 %fusion.45 = f32[256,6328]{1,0:T(8,128)S(1)} fusion(s32[6328]{0:T(1024)S(1)} %get-tuple-element.138, f32[1,112,256]{2,0,1:T(1,128)S(1)} %constant_dynamic-slice_fusion.2), kind=kOutput, calls=%fused_computation.5.clone.1 | convolution fusion | flops 2178654464 | bytes 6619872 | tf_op jit(solution)/shard_map/while/body/eval_jaxpr/dot_general | solution.py:65
  93.6 7.4 %convolution_multiply_fusion.2 = f32[256,6328]{1,0:T(8,128)S(1)} fusion(f32[256,6328]{1,0:T(8,128)S(1)} %fusion.45, s32[6328]{0:T(1024)S(1)} %get-tuple-element.139, f32[1,112,256]{2,0,1:T(1,128)S(1)} %constant_dynamic-slice_fusion.2), kind=kOutput, calls=%fused_computation.2.clone.1 | convolution fusion | flops 2180274432 | bytes 13099744 | tf_op jit(solution)/shard_map/while/body/eval_jaxpr/dot_general | solution.py:68
  100.9 5.7 %convolution_bitcast_fusion.2 = f32[1,28,256]{2,1,0:T(8,128)S(1)} fusion(f32[256,6328]{1,0:T(8,128)S(1)} %convolution_multiply_fusion.2, f32[6328,28]{0,1:T(8,128)S(1)} %get-tuple-element.137), kind=kOutput, calls=%fused_computation.10.clone.1 | convolution fusion | flops 544309248 | bytes 7217280 | tf_op jit(solution)/shard_map/while/body/eval_jaxpr/dot_general | solution.py:71
  107.0 7.2 %fusion.45 = f32[256,6328]{1,0:T(8,128)S(1)} fusion(s32[6328]{0:T(1024)S(1)} %get-tuple-element.138, f32[1,112,256]{2,0,1:T(1,128)S(1)} %constant_dynamic-slice_fusion.2), kind=kOutput, calls=%fused_computation.5.clone.1 | convolution fusion | flops 2178654464 | bytes 6619872 | tf_op jit(solution)/shard_map/while/body/eval_jaxpr/dot_general | solution.py:65
  114.1 7.4 %convolution_multiply_fusion.2 = f32[256,6328]{1,0:T(8,128)S(1)} fusion(f32[256,6328]{1,0:T(8,128)S(1)} %fusion.45, s32[6328]{0:T(1024)S(1)} %get-tuple-element.139, f32[1,112,256]{2,0,1:T(1,128)S(1)} %constant_dynamic-slice_fusion.2), kind=kOutput, calls=%fused_computation.2.clone.1 | convolution fusion | flops 2180274432 | bytes 13099744 | tf_op jit(solution)/shard_map/while/body/eval_jaxpr/dot_general | solution.py:68
  121.5 5.7 %convolution_bitcast_fusion.2 = f32[1,28,256]{2,1,0:T(8,128)S(1)} fusion(f32[256,6328]{1,0:T(8,128)S(1)} %convolution_multiply_fusion.2, f32[6328,28]{0,1:T(8,128)S(1)} %get-tuple-element.137), kind=kOutput, calls=%fused_computation.10.clone.1 | convolution fusion | flops 544309248 | bytes 7217280 | tf_op jit(solution)/shard_map/while/body/eval_jaxpr/dot_general | solution.py:71
  127.7 0.9 pad_maximum_fusion.1
  (44 shorter events, 4.0 us)
Async XLA Ops:
  0.0 21.4 %copy-start.1 = (f32[4,28,4,256]{3,2,1,0:T(4,128)S(1)}, f32[4,28,4,256]{3,2,1,0:T(4,128)}, u32[]{:S(2)}) copy-start(f32[4,28,4,256]{3,2,1,0:T(4,128)} %param.10) | copy-start | bytes 1376260
  0.0 18.2 %collective-permute-start = (f32[4,28,4,256]{3,2,1,0:T(4,128)}, f32[4,28,4,256]{3,2,1,0:T(4,128)S(1)}, u32[]{:S(2)}, u32[]{:S(2)}) collective-permute-start(f32[4,28,4,256]{3,2,1,0:T(4,128)} %param.10), channel_id=1, source_target_pairs={{0,4},{4,8},{8,12},{12,16},{16,20},{20,24},{24,28},{28,32},{32,36}... | collective-permute-start | bytes 1376264 | tf_op jit(solution)/shard_map/ppermute | solution.py:33
  2.1 18.0 %collective-permute-start.1 = (f32[4,28,4,256]{3,2,1,0:T(4,128)}, f32[4,28,4,256]{3,2,1,0:T(4,128)S(1)}, u32[]{:S(2)}, u32[]{:S(2)}) collective-permute-start(f32[4,28,4,256]{3,2,1,0:T(4,128)} %param.10), channel_id=1, source_target_pairs={{4,0},{8,4},{12,8},{16,12},{20,16},{24,20},{28,24},{32,28},{36,32}... | collective-permute-start | bytes 1376264 | tf_op jit(solution)/shard_map/ppermute | solution.py:34
  22.5 8.0 %copy-start.4 = (f32[4,256]{1,0:T(4,128)S(1)}, f32[4,256]{1,0:T(4,128)}, u32[]{:S(2)}) copy-start(f32[4,256]{1,0:T(4,128)} %param.15) | copy-start | bytes 12292
  22.5 16.4 %copy-start.6 = (f32[28]{0:T(128)S(1)}, f32[28]{0:T(128)}, u32[]{:S(2)}) copy-start(f32[28]{0:T(128)} %param.12) | copy-start | bytes 340
  22.5 16.4 %copy-start.2 = (s32[6328,2]{0,1:T(2,128)S(1)}, s32[6328,2]{0,1:T(2,128)}, u32[]{:S(2)}) copy-start(s32[6328,2]{0,1:T(2,128)} %param.16) | copy-start | bytes 151876
  22.5 22.3 %copy-start.3 = (f32[3,4,256]{2,1,0:T(4,128)S(1)}, f32[3,4,256]{2,1,0:T(4,128)}, u32[]{:S(2)}) copy-start(f32[3,4,256]{2,1,0:T(4,128)} %param.14) | copy-start | bytes 36868
  22.5 22.3 %copy-start.5 = (f32[4,256]{1,0:T(4,128)S(1)}, f32[4,256]{1,0:T(4,128)}, u32[]{:S(2)}) copy-start(f32[4,256]{1,0:T(4,128)} %param.13) | copy-start | bytes 12292
  22.5 22.3 %slice-start = ((f32[3,4,256]{2,1,0:T(4,128)}), f32[2,4,256]{2,1,0:T(4,128)S(1)}, s32[]{:S(2)}) async-start(f32[3,4,256]{2,1,0:T(4,128)} %param.14), calls=%async_computation.1 | async-start | bytes 16384 | tf_op jit(solution)/shard_map/slice | solution.py:96
  22.6 22.4 %copy-start = (f32[6328,28]{0,1:T(8,128)S(1)}, f32[6328,28]{0,1:T(8,128)}, u32[]{:S(2)}) copy-start(f32[6328,28]{0,1:T(8,128)} %param.17) | copy-start | bytes 2126212
  24.3 20.6 %all-to-all-start = ((f32[4,28,4,256]{3,2,1,0:T(4,128)}), f32[4,28,4,256]{3,2,1,0:T(4,128)S(1)}, u32[]{:S(2)}, u32[]{:S(2)}) async-start(f32[4,28,4,256]{3,2,1,0:T(4,128)} %broadcast_in_dim.42), calls=%async_computation | async-start | bytes 917504 | tf_op jit(solution)/shard_map/all_to_all | solution.py:12
  30.5 8.5 %collective-permute-start.2 = (f32[1,256]{1,0:T(1,128)S(1)}, f32[1,256]{1,0:T(1,128)S(1)}, u32[]{:S(2)}, u32[]{:S(2)}) collective-permute-start(f32[1,256]{1,0:T(1,128)S(1)} %get-tuple-element.77), channel_id=1, source_target_pairs={{4,0},{8,4},{12,8},{16,12},{20,16},{24,20},{28,24},{32,28},{36,32}... | collective-permute-start | bytes 3080 | tf_op jit(solution)/shard_map/ppermute | solution.py:34
  36.9 7.9 %collective-permute-start.3 = (f32[1,256]{1,0:T(1,128)S(1)}, f32[1,256]{1,0:T(1,128)S(1)}, u32[]{:S(2)}, u32[]{:S(2)}) collective-permute-start(f32[1,256]{1,0:T(1,128)S(1)} %get-tuple-element.78), channel_id=1, source_target_pairs={{0,4},{4,8},{8,12},{12,16},{16,20},{20,24},{24,28},{28,32},{32,36}... | collective-permute-start | bytes 3080 | tf_op jit(solution)/shard_map/ppermute | solution.py:33
where the time goes:
time: 129 us
  matrix products  80.9 us (63%)
  starting transfers between devices  28.3 us (22%)
  waiting for transfers between devices  11.4 us (9%)
  other arithmetic  5.17 us (4%)
  local copies, waits for them, and re-layouts  2.2 us (2%)
    dot_general x4, matrix products, one_block(): jnp.dot(second_hot, piece, precision=lax.Precision.HIGHEST, preferred_ele...  29.5 us
    dot_general x4, matrix products, one_block(): jnp.dot(first_hot, piece, precision=lax.Precision.HIGHEST, preferred_elem...  28.7 us
    dot_general x4, matrix products, one_block(): lax.dot_general(outcome, first_bins * second_bins, (((0,), (0,)), ((), ()...  22.7 us
    ppermute x2, starting transfers between devices, padded_2(): after = lax.ppermute(first, axis, down)  18.1 us
    ppermute x2, waiting for transfers between devices, padded_2(): before = lax.ppermute(last, axis, up)  9.55 us
    all_to_all x1, starting transfers between devices, from_everyone(): return lax.all_to_all(copies, axis, split_axis=0, concat_axis=0, tiled=True)  6.19 us
    ppermute x2, starting transfers between devices, padded_2(): before = lax.ppermute(last, axis, up)  3.96 us
  transfers between devices with their start and end apart: 5, of which 3 were waited for; matrix products, arithmetic and copies ran while one was open for 1% of the time, Pallas kernels for 0%

commit v1 on v0

v1 whole, which is shorter than its diff:
```python
import functools

import jax
import jax.numpy as jnp
from jax import lax
from jax.experimental import pallas as pl
from jax.experimental.pallas import tpu as pltpu
from jax.sharding import PartitionSpec as P

MESH = pl.DeviceIdType.MESH
BINS = 112
LOCAL = 28
PAIRS = 6328
PADDED = 6400
ZERO_ROW = PADDED - 1
GROUPS = 7
f32, bf16, i32 = jnp.float32, jnp.bfloat16, jnp.int32


def bin_at(group, member):
    if group < 6:
        tile = 2 * group + member // 8
        return tile // 3, (tile % 3) * 8 + member % 8
    return member // 4, 24 + member % 4


def group_member(index):
    shard = (index >= 28).astype(i32) + (index >= 56).astype(i32) + (index >= 84).astype(i32)
    own = index - 28 * shard
    tile = 3 * shard + (own >> 3)
    full = own < 24
    group = jnp.where(full, tile >> 1, 6)
    member = jnp.where(full, ((tile & 1) << 3) + (own & 7), 4 * shard + own - 24)
    return group, member


def slots_of(pairs):
    group_i, member_i = group_member(pairs[0:1, :])
    group_j, member_j = group_member(pairs[1:2, :])
    ahead = group_j - group_i
    ahead = jnp.where(ahead < 0, ahead + GROUPS, ahead)
    keep = ahead <= 3
    row = jnp.where(keep, group_i * 16 + member_i, group_j * 16 + member_j)
    slot = jnp.where(keep, ahead * 16 + member_j, (GROUPS - ahead) * 16 + member_i)
    return row, slot


def invert_pairs(pairs_ref, table_ref):
    total = jnp.zeros((BINS, 128), f32)
    for start in range(0, PAIRS, 256):
        width = min(256, PAIRS - start)
        row, slot = slots_of(pairs_ref[:, start : start + width])
        rows = lax.broadcasted_iota(i32, (BINS, width), 0)
        lanes = lax.broadcasted_iota(i32, (128, width), 0)
        number = start + 1 + lax.broadcasted_iota(i32, (1, width), 1)
        high = (number >> 6).astype(f32)
        low = (number & 63).astype(f32)
        value = jnp.where(lanes < 64, high, low)
        first = jnp.where(rows == row, 1.0, 0.0).astype(bf16)
        second = jnp.where((lanes & 63) == slot, value, 0.0).astype(bf16)
        total += lax.dot_general(first, second, (((1,), (1,)), ((), ())), preferred_element_type=f32)
    number = total * 64.0 + pltpu.roll(total, 64, 1)
    number = number.astype(i32)
    table_ref[...] = jnp.where(number > 0, number - 1, ZERO_ROW)


def turn_outcome(outcome_ref, turned_ref):
    for start in range(0, PAIRS, 128):
        width = min(128, PAIRS - start)
        turned_ref[start : start + width, 0:LOCAL] = outcome_ref[:, start : start + width].T
    turned_ref[PAIRS:PADDED, :] = jnp.zeros((PADDED - PAIRS, 128), f32)


def gather_two(table, turned_ref, held_ref, two):
    for half in range(2):
        for slot in range(64):
            at = half * 64 + slot
            index = table[2 * two + half, slot]
            held_ref[at : at + 1, :] = turned_ref[pl.ds(index, 1), :]


def place_two(held_ref, rates_ref, two):
    value = held_ref[...].T[0:32, :]
    high = value.astype(bf16).astype(f32)
    low = pltpu.roll(value - high, 64, 1)
    left = lax.broadcasted_iota(i32, (32, 128), 1) < 64
    start = pl.multiple_of(two * 64, 64)
    rates_ref[pl.ds(start, 32), :] = jnp.where(left, high, low).astype(bf16)
    rates_ref[pl.ds(start + 32, 32), :] = jnp.where(left, low, high).astype(bf16)


def sort_kernel(outcome_ref, pairs_ref, rates_ref, turned, held_a, held_b, table_v, table, sem):
    invert_pairs(pairs_ref, table_v)
    copy = pltpu.make_async_copy(table_v, table, sem)
    copy.start()
    turn_outcome(outcome_ref, turned)
    copy.wait()
    gather_two(table, turned, held_a, 0)

    def step(i, carry):
        gather_two(table, turned, held_b, 2 * i + 1)
        place_two(held_a, rates_ref, 2 * i)
        gather_two(table, turned, held_a, jnp.minimum(2 * i + 2, 55))
        place_two(held_b, rates_ref, 2 * i + 1)
        return carry

    lax.fori_loop(0, 28, step, 0)


def transported(own, before, after, speed):
    forward = jnp.maximum(speed, 0.0)
    backward = jnp.maximum(-speed, 0.0)

    def weights(a):
        square = a * a
        return (2.0 * a - 3.0 * square, 2.75 * square - 0.5 * a, -square, 0.125 * square)

    a = forward + backward
    row = lax.broadcasted_iota(i32, (8, 128), 0) & 3
    result = (1.0 - 1.5 * a + 1.125 * (a * a)) * own
    up, down = weights(forward), weights(backward)
    for m in (1, 2, 3):
        result += up[m - 1] * jnp.where(row >= m, pltpu.roll(own, m, 0), pltpu.roll(before, 4 + m, 0))
        result += down[m - 1] * jnp.where(row < 4 - m, pltpu.roll(own, 8 - m, 0), pltpu.roll(after, 4 - m, 0))
    return result + up[3] * before + down[3] * after


def step_kernel(
    dust, speed, stop, rho, vel, pres, rates, out,
    own, before, after, pres_before, pres_after, dens, high, low, source,
    own_sem, up_send, up_recv, down_send, down_recv, ring_send, ring_recv,
):
    tile, shard = lax.axis_index("tiles"), lax.axis_index("bins")
    tiles, shards = lax.axis_size("tiles"), lax.axis_size("bins")
    has_before, has_after = tile > 0, tile < tiles - 1
    nxt, prv = lax.rem(shard + 1, shards), lax.rem(shard + shards - 1, shards)

    own_copies = [
        pltpu.make_async_copy(dust.at[0:1], own.at[0:1], own_sem.at[0]),
        pltpu.make_async_copy(dust.at[1:4], own.at[1:4], own_sem.at[1]),
    ]
    for copy in own_copies:
        copy.start()

    barrier = pltpu.get_barrier_semaphore()
    pl.semaphore_signal(barrier, inc=1, device_id={"bins": nxt}, device_id_type=MESH)
    pl.semaphore_signal(barrier, inc=1, device_id={"bins": prv}, device_id_type=MESH)

    @pl.when(has_before)
    def _():
        pl.semaphore_signal(barrier, inc=1, device_id={"tiles": tile - 1}, device_id_type=MESH)

    @pl.when(has_after)
    def _():
        pl.semaphore_signal(barrier, inc=1, device_id={"tiles": tile + 1}, device_id_type=MESH)

    pl.semaphore_wait(barrier, 2 + has_before.astype(i32) + has_after.astype(i32))

    def tile_copies(send, recv, target, there, pres_there):
        make = functools.partial(pltpu.make_async_remote_copy, device_id={"tiles": target}, device_id_type=MESH)
        return [
            make(dust.at[0:1], there.at[0:1], send.at[0], recv.at[0]),
            make(pres, pres_there, send.at[1], recv.at[1]),
            make(dust.at[1:4], there.at[1:4], send.at[2], recv.at[2]),
        ]

    ups = tile_copies(up_send, up_recv, tile + 1, before, pres_before)
    downs = tile_copies(down_send, down_recv, tile - 1, after, pres_after)

    for part in range(3):
        @pl.when(has_after)
        def _():
            ups[part].start()

        @pl.when(has_before)
        def _():
            downs[part].start()

    @pl.when(jnp.logical_not(has_before))
    def _():
        before[...] = jnp.zeros_like(before)
        pres_before[...] = jnp.zeros_like(pres_before)

    @pl.when(jnp.logical_not(has_after))
    def _():
        after[...] = jnp.zeros_like(after)
        pres_after[...] = jnp.zeros_like(pres_after)

    def arrived(part):
        @pl.when(has_before)
        def _():
            ups[part].wait_recv()

        @pl.when(has_after)
        def _():
            downs[part].wait_recv()

    own_copies[0].wait()
    arrived(0)
    here = shard * 224
    for k in range(LOCAL):
        moved = transported(own[0, k], before[0, k], after[0, k], jnp.full((8, 128), speed[k], f32))
        out[0, k] = moved
        dens[pl.ds(here + k, 8, stride=LOCAL), :] = moved

    def ring_copy(block, half, target, slot):
        piece = dens.at[pl.ds(pl.multiple_of(block * 224 + half * 112, 16), 112), :]
        return pltpu.make_async_remote_copy(
            piece, piece, ring_send.at[slot], ring_recv.at[slot],
            device_id={"bins": target}, device_id_type=MESH,
        )

    two_back = lax.rem(shard + 2, shards)
    sends = [
        ring_copy(shard, 0, nxt, 0),
        ring_copy(shard, 1, prv, 1),
        ring_copy(shard, 1, nxt, 2),
        ring_copy(shard, 0, prv, 3),
    ]
    from_prv0 = ring_copy(prv, 0, nxt, 0)
    from_nxt1 = ring_copy(nxt, 1, prv, 1)
    from_prv1 = ring_copy(prv, 1, nxt, 2)
    from_nxt0 = ring_copy(nxt, 0, prv, 3)
    relay0 = ring_copy(prv, 0, nxt, 4)
    relay1 = ring_copy(nxt, 1, prv, 5)
    far0 = ring_copy(two_back, 0, nxt, 4)
    far1 = ring_copy(two_back, 1, prv, 5)
    for copy in sends:
        copy.start()

    own_copies[1].wait()
    arrived(1)
    arrived(2)

    def momenta(k, carry):
        rate = jnp.full((8, 128), speed[k], f32)
        for d in range(1, 4):
            out[d, k] = transported(own[d, k], before[d, k], after[d, k], rate)
        return carry

    lax.fori_loop(0, LOCAL, momenta, 0)

    from_prv0.wait_recv()
    relay0.start()
    from_nxt1.wait_recv()
    relay1.start()
    from_prv1.wait_recv()
    from_nxt0.wait_recv()
    far0.wait_recv()
    far1.wait_recv()

    for m in range(8):
        for group in range(GROUPS):
            if group < 6:
                starts = [bin_at(group, 0), bin_at(group, 8)]
                pieces = [dens[b * 224 + m * 28 + w : b * 224 + m * 28 + w + 8, :] for b, w in starts]
            else:
                pieces = [dens[b * 224 + m * 28 + 24 : b * 224 + m * 28 + 28, :] for b in range(4)]
            value = jnp.concatenate(pieces, 0)
            top = value.astype(bf16)
            rest = (value - top.astype(f32)).astype(bf16)
            for at in (group, group + GROUPS):
                if at < 10:
                    high[at * 16 : at * 16 + 16, m * 128 : m * 128 + 128] = top
                    low[at * 16 : at * 16 + 16, m * 128 : m * 128 + 128] = rest

    def columns(c, carry):
        cols = pl.ds(pl.multiple_of(c * 256, 256), 256)
        total = jnp.zeros((32, 256), f32)
        for group in range(GROUPS):
            window = pl.ds(group * 16, 64)
            top, rest = high[window, cols], low[window, cols]
            weights = jnp.concatenate([top, top, rest, rest], 0)
            block = rates[group * 512 : group * 512 + 512, :]
            product = jnp.dot(jnp.concatenate([block, block], 1), weights, preferred_element_type=f32)
            for member in range(16):
                b, w = bin_at(group, member)
                first = dens[pl.ds(b * 224 + w + c * 56, 1), :]
                second = dens[pl.ds(b * 224 + w + 28 + c * 56, 1), :]
                line = jnp.concatenate([first, second], 1)
                total += product[member * 32 : member * 32 + 32, :] * line
        for half in range(2):
            for k in range(4):
                source[pl.ds(k * 64 + 2 * c + half, 8, stride=8), :] = total[k * 8 : k * 8 + 8, half * 128 : half * 128 + 128]
        return carry

    lax.fori_loop(0, 4, columns, 0)

    row = lax.broadcasted_iota(i32, (8, 128), 0) & 3
    here_p = pres[...]
    above = jnp.where(row < 3, pltpu.roll(here_p, 7, 0), pltpu.roll(pres_after[...], 3, 0))
    below = jnp.where(row >= 1, pltpu.roll(here_p, 1, 0), pltpu.roll(pres_before[...], 5, 0))
    gradient = (above - below) / (2.0 * rho[...])
    gas = [vel[d] for d in range(3)]
    target = [gas[0] - gradient, gas[1], gas[2]]

    for k in range(LOCAL):
        half = 0.5 * source[k * 8 : k * 8 + 8, :]
        density = out[0, k] + half
        s = jnp.full((8, 128), stop[k], f32)
        share = 1.0 / (1.0 + s)
        pull = s * density
        out[0, k] = density
        for d in range(3):
            grown = out[d + 1, k] + half * gas[d]
            out[d + 1, k] = (grown + pull * target[d]) * share

    for copy in (*sends, relay0, relay1):
        copy.wait_send()
    for part in range(3):
        @pl.when(has_after)
        def _():
            ups[part].wait_send()

        @pl.when(has_before)
        def _():
            downs[part].wait_send()


VMEM_SPEC = pl.BlockSpec(memory_space=pltpu.VMEM)
SMEM_SPEC = pl.BlockSpec(memory_space=pltpu.SMEM)
ANY_SPEC = pl.BlockSpec(memory_space=pl.ANY)


def folded(value):
    lead = value.shape[:-2]
    value = value.reshape(*lead, 4, 2, 128)
    return jnp.swapaxes(value, -3, -2).reshape(*lead, 8, 128)


def unfolded(value):
    lead = value.shape[:-2]
    value = value.reshape(*lead, 2, 4, 128)
    return jnp.swapaxes(value, -3, -2).reshape(*lead, 4, 256)


def local(dust_state, drift_speed, stop_ratio, gas_rho, gas_vel, pressure, pair_list, outcome):
    rates = pl.pallas_call(
        sort_kernel,
        out_shape=jax.ShapeDtypeStruct((BINS * 32, 128), bf16),
        in_specs=[VMEM_SPEC, VMEM_SPEC],
        out_specs=VMEM_SPEC,
        scratch_shapes=[
            pltpu.VMEM((PADDED, 128), f32),
            pltpu.VMEM((128, 128), f32),
            pltpu.VMEM((128, 128), f32),
            pltpu.VMEM((BINS, 128), i32),
            pltpu.SMEM((BINS, 128), i32),
            pltpu.SemaphoreType.DMA,
        ],
        compiler_params=pltpu.CompilerParams(vmem_limit_bytes=24 << 20),
        name="sort_rates",
    )(outcome.T, pair_list.T)
    halo = pltpu.VMEM((4, LOCAL, 8, 128), f32)
    result = pl.pallas_call(
        step_kernel,
        out_shape=jax.ShapeDtypeStruct((4, LOCAL, 8, 128), f32),
        in_specs=[ANY_SPEC, SMEM_SPEC, SMEM_SPEC, VMEM_SPEC, VMEM_SPEC, VMEM_SPEC, VMEM_SPEC],
        out_specs=VMEM_SPEC,
        scratch_shapes=[
            halo, halo, halo,
            pltpu.VMEM((8, 128), f32),
            pltpu.VMEM((8, 128), f32),
            pltpu.VMEM((4 * 224, 128), f32),
            pltpu.VMEM((160, 1024), bf16),
            pltpu.VMEM((160, 1024), bf16),
            pltpu.VMEM((256, 128), f32),
            pltpu.SemaphoreType.DMA((2,)),
            pltpu.SemaphoreType.DMA((3,)),
            pltpu.SemaphoreType.DMA((3,)),
            pltpu.SemaphoreType.DMA((3,)),
            pltpu.SemaphoreType.DMA((3,)),
            pltpu.SemaphoreType.DMA((6,)),
            pltpu.SemaphoreType.DMA((6,)),
        ],
        compiler_params=pltpu.CompilerParams(
            collective_id=0, has_side_effects=True, vmem_limit_bytes=24 << 20
        ),
        name="dust_step",
    )(folded(dust_state), drift_speed, stop_ratio, folded(gas_rho), folded(gas_vel), folded(pressure), rates)
    return unfolded(result)


def solution(mesh):
    return jax.shard_map(
        local,
        mesh=mesh,
        in_specs=(
            P(None, "bins", "tiles", None),
            P("bins"),
            P("bins"),
            P("tiles", None),
            P(None, "tiles", None),
            P("tiles", None),
            P(),
            P(None, "bins"),
        ),
        out_specs=P(None, "bins", "tiles", None),
        check_vma=False,
    )
```

time: 129 us -> 49.7 us (0.39)
  matrix products: 80.9 us -> 0 us
  Pallas kernels: 0 us -> 46.7 us
  starting transfers between devices: 28.3 us -> 0 us
  waiting for transfers between devices: 11.4 us -> 0 us
  other arithmetic: 5.17 us -> 0 us
    dot_general x12 -> x0, matrix products: 80.9 us -> none  [the longest x4 29.5 us: one_block(): jnp.dot(second_hot, piece, precision=lax.Precision.HIGHEST, preferred_ele...]
    pallas_call x0 -> x2, Pallas kernels: none -> 46.7 us  [the longest x1 34.3 us: local(): pl.pallas_call(step_kernel, out_shape=jax.ShapeDtypeStruct((4, LOCAL, 8,...]
    ppermute x4 -> x0, starting transfers between devices: 22.1 us -> none  [the longest x2 18.1 us: padded_2(): after = lax.ppermute(first, axis, down)]
    ppermute x4 -> x0, waiting for transfers between devices: 11.4 us -> none  [the longest x2 9.55 us: padded_2(): before = lax.ppermute(last, axis, up)]
    all_to_all x1 -> x0, starting transfers between devices: 6.19 us -> none  [from_everyone(): return lax.all_to_all(copies, axis, split_axis=0, concat_axis=0, tiled=True)]
    unnamed x14 -> x17, local copies, waits for them, and re-layouts: 0.04 us -> 2.74 us
    concatenate x3 -> x0, other arithmetic: 2.22 us -> none  [the longest x1 1.34 us: padded_2(): value = jnp.concatenate([before, value, after], axis=dim)]
  transfers between devices with their start and end apart: 5 -> 0, of which waited for: 3 -> 0; matrix products, arithmetic and copies ran while one was open for 1% -> 0% of each run, Pallas kernels for 0% -> 0%
where the time goes in v1:
time: 49.7 us; the launch traced here: 49.5 us
  Pallas kernels  46.7 us (94%)
  local copies, waits for them, and re-layouts  2.74 us (6%)
    pallas_call x1, Pallas kernels, local(): pl.pallas_call(step_kernel, out_shape=jax.ShapeDtypeStruct((4, LOCAL, 8,...  34.3 us
    pallas_call x1, Pallas kernels, local(): pl.pallas_call(sort_kernel, out_shape=jax.ShapeDtypeStruct((BINS * 32, 12...  12.4 us
    unnamed x17, local copies, waits for them, and re-layouts  2.74 us

profile of v1, /device:TPU:6, one launch (start us, length us, event | category | flops | bytes accessed | tf_op | source)
XLA Modules:
  0.0 49.5 jit_solution(6013930991469967248)
XLA Ops:
  0.0 0.0 copy-start
  0.0 1.1 %copy-done = f32[6328,28]{0,1:T(8,128)S(1)} copy-done((f32[6328,28]{0,1:T(8,128)S(1)}, f32[6328,28]{0,1:T(8,128)}, u32[]{:S(2)}) %copy-start) | copy-done | bytes 708760
  1.1 0.0 copy-start.2
  1.1 0.8 %copy-done.2 = s32[6328,2]{0,1:T(2,128)S(1)} copy-done((s32[6328,2]{0,1:T(2,128)S(1)}, s32[6328,2]{0,1:T(2,128)}, u32[]{:S(2)}) %copy-start.2) | copy-done | bytes 50648
  1.9 0.0 copy-start.1
  2.0 0.0 copy-start.3
  2.0 0.0 copy-start.4
  2.0 0.0 copy-start.5
  2.0 0.0 copy-start.6
  2.0 0.0 copy-start.7
  2.0 12.4 %sort_rates.1.rates = bf16[3584,128]{1,0:T(8,128)(2,1)S(1)} custom-call(f32[28,6328]{1,0:T(8,128)S(1)} %bitcast.28, s32[2,6328]{1,0:T(2,128)S(1)} %bitcast.30), custom_call_target="tpu_custom_call" | custom-call | tf_op jit(solution)/shard_map/sort_rates/pallas_call | solution.py:338
  14.4 0.0 copy-done.1
  14.4 0.0 copy-done.3
  14.4 0.0 copy-done.4
  14.5 0.0 copy-done.5
  14.5 0.0 copy-done.6
  14.5 0.0 copy-done.7
  14.5 34.3 %dust_step.1 = f32[4,28,8,128]{3,2,1,0:T(8,128)S(1)} custom-call(f32[4,28,8,128]{3,2,1,0:T(8,128)S(1)} %bitcast.29, f32[28]{0:T(128)S(1)} %copy-done.6, f32[28]{0:T(128)S(1)} %copy-done.7, f32[8,128]{1,0:T(8,128)S(1)} %bitcast.32, f32[3,8,128]{2,1,0:T(8,128)S(1)} %bitcast.31, f32[8,128]{1,0:T(8,128)S(1)} %bitcast.33, bf16[3584,128]{1,0:T(8,128)(2,1)S(1)} %sort_rates.1.rates), custom_call_target="tpu_custom_call" | custom-call | tf_op jit(solution)/shard_map/dust_step/pallas_call | solution.py:355
  48.8 0.8 %copy.15 = f32[4,28,4,256]{3,2,1,0:T(4,128)} copy(f32[4,28,4,256]{3,2,1,0:T(4,128)S(1)} %bitcast.27) | data formatting | bytes 917504
Async XLA Ops:
  0.0 1.1 %copy-start = (f32[6328,28]{0,1:T(8,128)S(1)}, f32[6328,28]{0,1:T(8,128)}, u32[]{:S(2)}) copy-start(f32[6328,28]{0,1:T(8,128)} %param.15) | copy-start | bytes 2126212
  1.1 0.8 %copy-start.2 = (s32[6328,2]{0,1:T(2,128)S(1)}, s32[6328,2]{0,1:T(2,128)}, u32[]{:S(2)}) copy-start(s32[6328,2]{0,1:T(2,128)} %param.14) | copy-start | bytes 151876
  1.9 12.5 %copy-start.1 = (f32[4,28,4,256]{3,2,1,0:T(4,128)S(1)}, f32[4,28,4,256]{3,2,1,0:T(4,128)}, u32[]{:S(2)}) copy-start(f32[4,28,4,256]{3,2,1,0:T(4,128)} %param.8) | copy-start | bytes 1376260
  2.0 12.5 %copy-start.3 = (f32[3,4,256]{2,1,0:T(4,128)S(1)}, f32[3,4,256]{2,1,0:T(4,128)}, u32[]{:S(2)}) copy-start(f32[3,4,256]{2,1,0:T(4,128)} %param.12) | copy-start | bytes 36868
  2.0 12.5 %copy-start.4 = (f32[4,256]{1,0:T(4,128)S(1)}, f32[4,256]{1,0:T(4,128)}, u32[]{:S(2)}) copy-start(f32[4,256]{1,0:T(4,128)} %param.11) | copy-start | bytes 12292
  2.0 12.5 %copy-start.5 = (f32[4,256]{1,0:T(4,128)S(1)}, f32[4,256]{1,0:T(4,128)}, u32[]{:S(2)}) copy-start(f32[4,256]{1,0:T(4,128)} %param.13) | copy-start | bytes 12292
  2.0 12.5 %copy-start.6 = (f32[28]{0:T(128)S(1)}, f32[28]{0:T(128)}, u32[]{:S(2)}) copy-start(f32[28]{0:T(128)} %speed.1) | copy-start | bytes 340
  2.0 12.5 %copy-start.7 = (f32[28]{0:T(128)S(1)}, f32[28]{0:T(128)}, u32[]{:S(2)}) copy-start(f32[28]{0:T(128)} %stop.1) | copy-start | bytes 340

commit v2 on v1

v2 whole, which is shorter than its diff:
```python
import functools

import jax
import jax.numpy as jnp
from jax import lax
from jax.experimental import pallas as pl
from jax.experimental.pallas import tpu as pltpu
from jax.sharding import PartitionSpec as P

MESH = pl.DeviceIdType.MESH
BINS = 112
LOCAL = 28
PAIRS = 6328
GROUPS = 7
f32, bf16, i32 = jnp.float32, jnp.bfloat16, jnp.int32


def bin_at(group, member):
    if group < 6:
        tile = 2 * group + member // 8
        return tile // 3, (tile % 3) * 8 + member % 8
    return member // 4, 24 + member % 4


def group_member(index):
    shard = (index >= 28).astype(i32) + (index >= 56).astype(i32) + (index >= 84).astype(i32)
    own = index - 28 * shard
    tile = 3 * shard + (own >> 3)
    full = own < 24
    group = jnp.where(full, tile >> 1, 6)
    member = jnp.where(full, ((tile & 1) << 3) + (own & 7), 4 * shard + own - 24)
    return group, member


def slots_of(pairs):
    group_i, member_i = group_member(pairs[0:1, :])
    group_j, member_j = group_member(pairs[1:2, :])
    ahead = group_j - group_i
    ahead = jnp.where(ahead < 0, ahead + GROUPS, ahead)
    keep = ahead <= 3
    row = jnp.where(keep, group_i * 16 + member_i, group_j * 16 + member_j)
    slot = jnp.where(keep, ahead * 16 + member_j, (GROUPS - ahead) * 16 + member_i)
    return row, slot


def invert_pairs(pairs_ref, table_ref):
    total = jnp.zeros((BINS, 128), f32)
    for start in range(0, PAIRS, 256):
        width = min(256, PAIRS - start)
        row, slot = slots_of(pairs_ref[:, start : start + width])
        rows = lax.broadcasted_iota(i32, (BINS, width), 0)
        lanes = lax.broadcasted_iota(i32, (128, width), 0)
        number = start + 1 + lax.broadcasted_iota(i32, (1, width), 1)
        high = (number >> 6).astype(f32)
        low = (number & 63).astype(f32)
        value = jnp.where(lanes < 64, high, low)
        first = jnp.where(rows == row, 1.0, 0.0).astype(bf16)
        second = jnp.where((lanes & 63) == slot, value, 0.0).astype(bf16)
        total += lax.dot_general(first, second, (((1,), (1,)), ((), ())), preferred_element_type=f32)
    number = total * 64.0 + pltpu.roll(total, 64, 1)
    table_ref[...] = jnp.clip(number.astype(i32) - 1, 0, PAIRS - 1)


def turn_outcome(outcome_ref, turned_ref):
    for start in range(0, PAIRS, 128):
        width = min(128, PAIRS - start)
        turned_ref[start : start + width, 0:LOCAL] = outcome_ref[:, start : start + width].T


def gather_two(table, turned, held, two):
    for half in range(2):
        member = 2 * two + half
        for slot in range(member, 64):
            at = half * 64 + slot
            index = table[member % 8, slot]
            held[at : at + 1, :] = turned[pl.ds(index, 1), :]


def place_two(held, rates, group, two):
    lane = lax.broadcasted_iota(i32, (32, 128), 1)
    left = lane < 64
    unused = (lane < 2 * two) | ((lane >= 64) & (lane < 64 + 2 * two + 1))
    value = jnp.where(unused, 0.0, held[...].T[0:32, :])
    high = value.astype(bf16).astype(f32)
    low = pltpu.roll(value - high, 64, 1)
    start = pl.multiple_of(group * 512 + two * 64, 64)
    rates[pl.ds(start, 32), :] = jnp.where(left, high, low).astype(bf16)
    rates[pl.ds(start + 32, 32), :] = jnp.where(left, low, high).astype(bf16)


def sort_kernel(pairs_in, outcome_in, rates, pairs, outcome, turned, held, table_v, table_a, table_b, in_sem, table_sem):
    pairs_copy = pltpu.make_async_copy(pairs_in, pairs, in_sem.at[0])
    outcome_copy = pltpu.make_async_copy(outcome_in, outcome, in_sem.at[1])
    pairs_copy.start()
    outcome_copy.start()

    def table_copy(group, half):
        rows = pl.ds(pl.multiple_of(group * 16 + half * 8, 8), 8)
        return pltpu.make_async_copy(table_v.at[rows, :], (table_a, table_b)[half], table_sem.at[half])

    pairs_copy.wait()
    invert_pairs(pairs, table_v)
    table_copy(0, 0).start()
    table_copy(0, 1).start()
    outcome_copy.wait()
    turn_outcome(outcome, turned)

    def sort_group(group, carry):
        for half in range(2):
            table_copy(group, half).wait()
            for two in range(4 * half, 4 * half + 4):
                gather_two((table_a, table_b)[half], turned, held.at[two], two)
                place_two(held.at[two], rates, group, two)

            @pl.when(group < GROUPS - 1)
            def _():
                table_copy(jnp.minimum(group + 1, GROUPS - 1), half).start()

        return carry

    lax.fori_loop(0, GROUPS, sort_group, 0)


def transported(own, before, after, speed):
    forward = jnp.maximum(speed, 0.0)
    backward = jnp.maximum(-speed, 0.0)

    def weights(a):
        square = a * a
        return (2.0 * a - 3.0 * square, 2.75 * square - 0.5 * a, -square, 0.125 * square)

    a = forward + backward
    row = lax.broadcasted_iota(i32, (8, 128), 0) & 3
    result = (1.0 - 1.5 * a + 1.125 * (a * a)) * own
    up, down = weights(forward), weights(backward)
    for m in (1, 2, 3):
        result += up[m - 1] * jnp.where(row >= m, pltpu.roll(own, m, 0), pltpu.roll(before, 4 + m, 0))
        result += down[m - 1] * jnp.where(row < 4 - m, pltpu.roll(own, 8 - m, 0), pltpu.roll(after, 4 - m, 0))
    return result + up[3] * before + down[3] * after


def step_kernel(
    dust_in, speed, stop, rho, vel, pres, rates, out,
    own, before, after, pres_before, pres_after, dens, high, low, source,
    own_sem, up_send, up_recv, down_send, down_recv, ring_send, ring_recv,
):
    tile, shard = lax.axis_index("tiles"), lax.axis_index("bins")
    tiles, shards = lax.axis_size("tiles"), lax.axis_size("bins")
    has_before, has_after = tile > 0, tile < tiles - 1
    nxt, prv = lax.rem(shard + 1, shards), lax.rem(shard + shards - 1, shards)

    barrier = pltpu.get_barrier_semaphore()
    pl.semaphore_signal(barrier, inc=1, device_id={"bins": nxt}, device_id_type=MESH)
    pl.semaphore_signal(barrier, inc=1, device_id={"bins": prv}, device_id_type=MESH)

    @pl.when(has_before)
    def _():
        pl.semaphore_signal(barrier, inc=1, device_id={"tiles": tile - 1}, device_id_type=MESH)

    @pl.when(has_after)
    def _():
        pl.semaphore_signal(barrier, inc=1, device_id={"tiles": tile + 1}, device_id_type=MESH)

    own_copies = [
        pltpu.make_async_copy(dust_in.at[0:1], own.at[0:1], own_sem.at[0]),
        pltpu.make_async_copy(dust_in.at[1:4], own.at[1:4], own_sem.at[1]),
    ]
    own_copies[0].start()
    own_copies[1].start()

    pl.semaphore_wait(barrier, 2 + has_before.astype(i32) + has_after.astype(i32))

    def tile_copies(send, recv, target, there, pres_there):
        make = functools.partial(pltpu.make_async_remote_copy, device_id={"tiles": target}, device_id_type=MESH)
        return [
            make(dust_in.at[0:1], there.at[0:1], send.at[0], recv.at[0]),
            make(pres, pres_there, send.at[1], recv.at[1]),
            make(dust_in.at[1:4], there.at[1:4], send.at[2], recv.at[2]),
        ]

    ups = tile_copies(up_send, up_recv, tile + 1, before, pres_before)
    downs = tile_copies(down_send, down_recv, tile - 1, after, pres_after)

    for part in range(3):
        @pl.when(has_after)
        def _():
            ups[part].start()

        @pl.when(has_before)
        def _():
            downs[part].start()

    @pl.when(jnp.logical_not(has_before))
    def _():
        before[...] = jnp.zeros_like(before)
        pres_before[...] = jnp.zeros_like(pres_before)

    @pl.when(jnp.logical_not(has_after))
    def _():
        after[...] = jnp.zeros_like(after)
        pres_after[...] = jnp.zeros_like(pres_after)

    def arrived(part):
        @pl.when(has_before)
        def _():
            ups[part].wait_recv()

        @pl.when(has_after)
        def _():
            downs[part].wait_recv()

    own_copies[0].wait()
    arrived(0)
    here = shard * 224
    for k in range(LOCAL):
        moved = transported(own[0, k], before[0, k], after[0, k], jnp.full((8, 128), speed[k], f32))
        out[0, k] = moved
        dens[pl.ds(here + k, 8, stride=LOCAL), :] = moved

    def ring_copy(block, chunk, target, slot):
        piece = dens.at[pl.ds(pl.multiple_of(block * 224 + chunk * 56, 8), 56), :]
        return pltpu.make_async_remote_copy(
            piece, piece, ring_send.at[slot], ring_recv.at[slot],
            device_id={"bins": target}, device_id_type=MESH,
        )

    two_back = lax.rem(shard + 2, shards)
    forward, backward, relayed = (0, 1, 2, 3), (2, 3, 0, 1), (0, 2, 1, 3)
    sends = []
    for i in range(4):
        sends.append(ring_copy(shard, forward[i], nxt, forward[i]))
        sends.append(ring_copy(shard, backward[i], prv, 4 + backward[i]))
    for copy in sends:
        copy.start()
    from_prv = [ring_copy(prv, c, nxt, c) for c in range(4)]
    from_nxt = [ring_copy(nxt, c, prv, 4 + c) for c in range(4)]
    relays = [ring_copy(prv, c, nxt, 8 + c) if c < 2 else ring_copy(nxt, c, prv, 8 + c) for c in range(4)]
    far = [ring_copy(two_back, c, nxt if c < 2 else prv, 8 + c) for c in range(4)]

    def relay(c):
        (from_prv if c < 2 else from_nxt)[c].wait_recv()
        relays[c].start()

    def momenta(k, carry):
        rate = jnp.full((8, 128), speed[k], f32)
        for d in range(1, 4):
            out[d, k] = transported(own[d, k], before[d, k], after[d, k], rate)
        return carry

    relay(0)
    relay(2)
    own_copies[1].wait()
    arrived(1)
    arrived(2)
    lax.fori_loop(0, LOCAL, momenta, 0)
    relay(1)
    relay(3)

    for c in range(2):
        from_prv[2 + c].wait_recv()
        from_nxt[c].wait_recv()

    for c in relayed:
        far[c].wait_recv()
        for m in (2 * c, 2 * c + 1):
            for group in range(GROUPS):
                if group < 6:
                    starts = [bin_at(group, 0), bin_at(group, 8)]
                    pieces = [dens[b * 224 + m * 28 + w : b * 224 + m * 28 + w + 8, :] for b, w in starts]
                else:
                    pieces = [dens[b * 224 + m * 28 + 24 : b * 224 + m * 28 + 28, :] for b in range(4)]
                value = jnp.concatenate(pieces, 0)
                top = value.astype(bf16)
                rest = (value - top.astype(f32)).astype(bf16)
                for at in (group, group + GROUPS):
                    if at < 10:
                        high[at * 16 : at * 16 + 16, m * 128 : m * 128 + 128] = top
                        low[at * 16 : at * 16 + 16, m * 128 : m * 128 + 128] = rest
        total = jnp.zeros((32, 256), f32)
        for group in range(GROUPS):
            top = high[group * 16 : group * 16 + 64, c * 256 : c * 256 + 256]
            rest = low[group * 16 : group * 16 + 64, c * 256 : c * 256 + 256]
            weights = jnp.concatenate([top, top, rest, rest], 0)
            block = rates[group * 512 : group * 512 + 512, :]
            product = jnp.dot(jnp.concatenate([block, block], 1), weights, preferred_element_type=f32)
            for member in range(16):
                b, w = bin_at(group, member)
                start = b * 224 + w + c * 56
                line = jnp.concatenate([dens[start : start + 1, :], dens[start + 28 : start + 29, :]], 1)
                total += product[member * 32 : member * 32 + 32, :] * line
        for half in range(2):
            for k in range(4):
                source[pl.ds(k * 64 + 2 * c + half, 8, stride=8), :] = total[k * 8 : k * 8 + 8, half * 128 : half * 128 + 128]

    row = lax.broadcasted_iota(i32, (8, 128), 0) & 3
    here_p = pres[...]
    above = jnp.where(row < 3, pltpu.roll(here_p, 7, 0), pltpu.roll(pres_after[...], 3, 0))
    below = jnp.where(row >= 1, pltpu.roll(here_p, 1, 0), pltpu.roll(pres_before[...], 5, 0))
    gradient = (above - below) / (2.0 * rho[...])
    gas = [vel[d] for d in range(3)]
    target = [gas[0] - gradient, gas[1], gas[2]]

    for k in range(LOCAL):
        half = 0.5 * source[k * 8 : k * 8 + 8, :]
        density = out[0, k] + half
        s = jnp.full((8, 128), stop[k], f32)
        share = 1.0 / (1.0 + s)
        pull = s * density
        out[0, k] = density
        for d in range(3):
            grown = out[d + 1, k] + half * gas[d]
            out[d + 1, k] = (grown + pull * target[d]) * share

    for copy in (*sends, *relays):
        copy.wait_send()
    for part in range(3):
        @pl.when(has_after)
        def _():
            ups[part].wait_send()

        @pl.when(has_before)
        def _():
            downs[part].wait_send()


def folded(value):
    lead = value.shape[:-2]
    value = value.reshape(*lead, 4, 2, 128)
    return jnp.swapaxes(value, -3, -2).reshape(*lead, 8, 128)


def unfolded(value):
    lead = value.shape[:-2]
    value = value.reshape(*lead, 2, 4, 128)
    return jnp.swapaxes(value, -3, -2).reshape(*lead, 4, 256)


def local(dust_state, drift_speed, stop_ratio, gas_rho, gas_vel, pressure, pair_list, outcome):
    dma = pltpu.SemaphoreType.DMA
    in_hbm = pl.BlockSpec(memory_space=pltpu.HBM)
    in_vmem = pl.BlockSpec(memory_space=pltpu.VMEM)
    in_smem = pl.BlockSpec(memory_space=pltpu.SMEM)
    rates = pl.pallas_call(
        sort_kernel,
        out_shape=jax.ShapeDtypeStruct((BINS * 32, 128), bf16),
        in_specs=[in_hbm, in_hbm],
        out_specs=in_vmem,
        scratch_shapes=[
            pltpu.VMEM((2, PAIRS), i32),
            pltpu.VMEM((LOCAL, PAIRS), f32),
            pltpu.VMEM((PAIRS, 128), f32),
            pltpu.VMEM((8, 128, 128), f32),
            pltpu.VMEM((BINS, 128), i32),
            pltpu.SMEM((8, 128), i32),
            pltpu.SMEM((8, 128), i32),
            dma((2,)), dma((2,)),
        ],
        compiler_params=pltpu.CompilerParams(vmem_limit_bytes=24 << 20),
        name="sort_rates",
    )(pair_list.T, outcome.T)
    halo = pltpu.VMEM((4, LOCAL, 8, 128), f32)
    cell = pltpu.VMEM((8, 128), f32)
    result = pl.pallas_call(
        step_kernel,
        out_shape=jax.ShapeDtypeStruct((4, LOCAL, 8, 128), f32),
        in_specs=[pl.BlockSpec(memory_space=pl.ANY), in_smem, in_smem, in_vmem, in_vmem, in_vmem, in_vmem],
        out_specs=in_vmem,
        scratch_shapes=[
            halo, halo, halo, cell, cell,
            pltpu.VMEM((4 * 224, 128), f32),
            pltpu.VMEM((160, 1024), bf16),
            pltpu.VMEM((160, 1024), bf16),
            pltpu.VMEM((256, 128), f32),
            dma((2,)), dma((3,)), dma((3,)), dma((3,)), dma((3,)),
            dma((12,)), dma((12,)),
        ],
        compiler_params=pltpu.CompilerParams(collective_id=0, has_side_effects=True, vmem_limit_bytes=24 << 20),
        name="dust_step",
    )(folded(dust_state), drift_speed, stop_ratio, folded(gas_rho), folded(gas_vel), folded(pressure), rates)
    return unfolded(result)


def solution(mesh):
    return jax.shard_map(
        local,
        mesh=mesh,
        in_specs=(
            P(None, "bins", "tiles", None),
            P("bins"),
            P("bins"),
            P("tiles", None),
            P(None, "tiles", None),
            P("tiles", None),
            P(),
            P(None, "bins"),
        ),
        out_specs=P(None, "bins", "tiles", None),
        check_vma=False,
    )
```

time: 49.7 us -> 45.7 us (0.920)
  Pallas kernels: 46.7 us -> 42.6 us
    pallas_call x1, Pallas kernels: 12.4 us -> 8.7 us  [local(): pl.pallas_call(sort_kernel, out_shape=jax.ShapeDtypeStruct((BINS * 32, 12...]
where the time goes in v2:
time: 45.7 us; the launch traced here: 45.5 us
  Pallas kernels  42.6 us (93%)
  local copies, waits for them, and re-layouts  2.74 us (6%)
    pallas_call x1, Pallas kernels, local(): pl.pallas_call(step_kernel, out_shape=jax.ShapeDtypeStruct((4, LOCAL, 8,...  33.9 us
    pallas_call x1, Pallas kernels, local(): pl.pallas_call(sort_kernel, out_shape=jax.ShapeDtypeStruct((BINS * 32, 12...  8.7 us
    unnamed x17, local copies, waits for them, and re-layouts  2.74 us

profile of v2, /device:TPU:6, one launch (start us, length us, event | category | flops | bytes accessed | tf_op | source)
XLA Modules:
  0.0 45.5 jit_solution(1660451484905259741)
XLA Ops:
  0.0 0.0 copy-start
  0.0 1.1 %copy-done = f32[6328,28]{0,1:T(8,128)S(1)} copy-done((f32[6328,28]{0,1:T(8,128)S(1)}, f32[6328,28]{0,1:T(8,128)}, u32[]{:S(2)}) %copy-start) | copy-done | bytes 708760
  1.1 0.0 copy-start.2
  1.1 0.8 %copy-done.2 = s32[6328,2]{0,1:T(2,128)S(1)} copy-done((s32[6328,2]{0,1:T(2,128)S(1)}, s32[6328,2]{0,1:T(2,128)}, u32[]{:S(2)}) %copy-start.2) | copy-done | bytes 50648
  1.9 0.0 copy-start.1
  2.0 0.0 copy-start.3
  2.0 0.0 copy-start.4
  2.0 0.0 copy-start.5
  2.0 0.0 copy-start.6
  2.0 0.0 copy-start.7
  2.0 8.7 %sort_rates.1.rates = bf16[3584,128]{1,0:T(8,128)(2,1)S(1)} custom-call(s32[2,6328]{1,0:T(2,128)S(1)} %bitcast.30, f32[28,6328]{1,0:T(8,128)S(1)} %bitcast.28), custom_call_target="tpu_custom_call" | custom-call | tf_op jit(solution)/shard_map/sort_rates/pallas_call | solution.py:343
  10.7 0.0 copy-done.1
  10.7 0.0 copy-done.3
  10.7 0.0 copy-done.4
  10.7 0.0 copy-done.5
  10.7 0.0 copy-done.6
  10.7 0.0 copy-done.7
  10.8 33.9 %dust_step.1 = f32[4,28,8,128]{3,2,1,0:T(8,128)S(1)} custom-call(f32[4,28,8,128]{3,2,1,0:T(8,128)S(1)} %bitcast.29, f32[28]{0:T(128)S(1)} %copy-done.6, f32[28]{0:T(128)S(1)} %copy-done.7, f32[8,128]{1,0:T(8,128)S(1)} %bitcast.32, f32[3,8,128]{2,1,0:T(8,128)S(1)} %bitcast.31, f32[8,128]{1,0:T(8,128)S(1)} %bitcast.33, bf16[3584,128]{1,0:T(8,128)(2,1)S(1)} %sort_rates.1.rates), custom_call_target="tpu_custom_call" | custom-call | tf_op jit(solution)/shard_map/dust_step/pallas_call | solution.py:363
  44.7 0.8 %copy.15 = f32[4,28,4,256]{3,2,1,0:T(4,128)} copy(f32[4,28,4,256]{3,2,1,0:T(4,128)S(1)} %bitcast.27) | data formatting | bytes 917504
Async XLA Ops:
  0.0 1.1 %copy-start = (f32[6328,28]{0,1:T(8,128)S(1)}, f32[6328,28]{0,1:T(8,128)}, u32[]{:S(2)}) copy-start(f32[6328,28]{0,1:T(8,128)} %param.15) | copy-start | bytes 2126212
  1.1 0.8 %copy-start.2 = (s32[6328,2]{0,1:T(2,128)S(1)}, s32[6328,2]{0,1:T(2,128)}, u32[]{:S(2)}) copy-start(s32[6328,2]{0,1:T(2,128)} %param.14) | copy-start | bytes 151876
  1.9 8.7 %copy-start.1 = (f32[4,28,4,256]{3,2,1,0:T(4,128)S(1)}, f32[4,28,4,256]{3,2,1,0:T(4,128)}, u32[]{:S(2)}) copy-start(f32[4,28,4,256]{3,2,1,0:T(4,128)} %param.8) | copy-start | bytes 1376260
  2.0 8.8 %copy-start.3 = (f32[3,4,256]{2,1,0:T(4,128)S(1)}, f32[3,4,256]{2,1,0:T(4,128)}, u32[]{:S(2)}) copy-start(f32[3,4,256]{2,1,0:T(4,128)} %param.12) | copy-start | bytes 36868
  2.0 8.8 %copy-start.4 = (f32[4,256]{1,0:T(4,128)S(1)}, f32[4,256]{1,0:T(4,128)}, u32[]{:S(2)}) copy-start(f32[4,256]{1,0:T(4,128)} %param.11) | copy-start | bytes 12292
  2.0 8.8 %copy-start.5 = (f32[4,256]{1,0:T(4,128)S(1)}, f32[4,256]{1,0:T(4,128)}, u32[]{:S(2)}) copy-start(f32[4,256]{1,0:T(4,128)} %param.13) | copy-start | bytes 12292
  2.0 8.8 %copy-start.6 = (f32[28]{0:T(128)S(1)}, f32[28]{0:T(128)}, u32[]{:S(2)}) copy-start(f32[28]{0:T(128)} %speed.1) | copy-start | bytes 340
  2.0 8.8 %copy-start.7 = (f32[28]{0:T(128)S(1)}, f32[28]{0:T(128)}, u32[]{:S(2)}) copy-start(f32[28]{0:T(128)} %stop.1) | copy-start | bytes 340

commit v3 on v2

--- a/solution.py
+++ b/solution.py
@@ -88,39 +88,6 @@
     rates[pl.ds(start + 32, 32), :] = jnp.where(left, low, high).astype(bf16)
 
 
-def sort_kernel(pairs_in, outcome_in, rates, pairs, outcome, turned, held, table_v, table_a, table_b, in_sem, table_sem):
-    pairs_copy = pltpu.make_async_copy(pairs_in, pairs, in_sem.at[0])
-    outcome_copy = pltpu.make_async_copy(outcome_in, outcome, in_sem.at[1])
-    pairs_copy.start()
-    outcome_copy.start()
-
-    def table_copy(group, half):
-        rows = pl.ds(pl.multiple_of(group * 16 + half * 8, 8), 8)
-        return pltpu.make_async_copy(table_v.at[rows, :], (table_a, table_b)[half], table_sem.at[half])
-
-    pairs_copy.wait()
-    invert_pairs(pairs, table_v)
-    table_copy(0, 0).start()
-    table_copy(0, 1).start()
-    outcome_copy.wait()
-    turn_outcome(outcome, turned)
-
-    def sort_group(group, carry):
-        for half in range(2):
-            table_copy(group, half).wait()
-            for two in range(4 * half, 4 * half + 4):
-                gather_two((table_a, table_b)[half], turned, held.at[two], two)
-                place_two(held.at[two], rates, group, two)
-
-            @pl.when(group < GROUPS - 1)
-            def _():
-                table_copy(jnp.minimum(group + 1, GROUPS - 1), half).start()
-
-        return carry
-
-    lax.fori_loop(0, GROUPS, sort_group, 0)
-
-
 def transported(own, before, after, speed):
     forward = jnp.maximum(speed, 0.0)
     backward = jnp.maximum(-speed, 0.0)
@@ -140,9 +107,11 @@
 
 
 def step_kernel(
-    dust_in, speed, stop, rho, vel, pres, rates, out,
+    dust_in, speed_in, stop_in, rho_in, vel_in, pres_in, pairs_in, outcome_in, out,
     own, before, after, pres_before, pres_after, dens, high, low, source,
-    own_sem, up_send, up_recv, down_send, down_recv, ring_send, ring_recv,
+    speed, stop, rho, vel, pres, pairs, outcome,
+    turned, held, table_v, table_a, table_b, rates,
+    own_sem, in_sem, table_sem, up_send, up_recv, down_send, down_recv, ring_send, ring_recv,
 ):
     tile, shard = lax.axis_index("tiles"), lax.axis_index("bins")
     tiles, shards = lax.axis_size("tiles"), lax.axis_size("bins")
@@ -165,8 +134,17 @@
         pltpu.make_async_copy(dust_in.at[0:1], own.at[0:1], own_sem.at[0]),
         pltpu.make_async_copy(dust_in.at[1:4], own.at[1:4], own_sem.at[1]),
     ]
+    moves = ((pairs_in, pairs), (speed_in, speed), (outcome_in, outcome), (stop_in, stop), (rho_in, rho), (vel_in, vel), (pres_in, pres))
+    pairs_copy, speed_copy, outcome_copy, *late_copies = [
+        pltpu.make_async_copy(source_ref, target_ref, in_sem.at[i]) for i, (source_ref, target_ref) in enumerate(moves)
+    ]
+    pairs_copy.start()
     own_copies[0].start()
+    speed_copy.start()
+    outcome_copy.start()
     own_copies[1].start()
+    for copy in late_copies:
+        copy.start()
 
     pl.semaphore_wait(barrier, 2 + has_before.astype(i32) + has_after.astype(i32))
 
@@ -174,7 +152,7 @@
         make = functools.partial(pltpu.make_async_remote_copy, device_id={"tiles": target}, device_id_type=MESH)
         return [
             make(dust_in.at[0:1], there.at[0:1], send.at[0], recv.at[0]),
-            make(pres, pres_there, send.at[1], recv.at[1]),
+            make(pres_in, pres_there, send.at[1], recv.at[1]),
             make(dust_in.at[1:4], there.at[1:4], send.at[2], recv.at[2]),
         ]
 
@@ -209,7 +187,20 @@
         def _():
             downs[part].wait_recv()
 
+    pairs_copy.wait()
+    invert_pairs(pairs, table_v)
+
+    def table_copy(group, half):
+        rows = pl.ds(pl.multiple_of(group * 16 + half * 8, 8), 8)
+        return pltpu.make_async_copy(table_v.at[rows, :], (table_a, table_b)[half], table_sem.at[half])
+
+    table_copy(0, 0).start()
+    table_copy(0, 1).start()
+    outcome_copy.wait()
+    turn_outcome(outcome, turned)
+
     own_copies[0].wait()
+    speed_copy.wait()
     arrived(0)
     here = shard * 224
     for k in range(LOCAL):
@@ -237,9 +228,38 @@
     relays = [ring_copy(prv, c, nxt, 8 + c) if c < 2 else ring_copy(nxt, c, prv, 8 + c) for c in range(4)]
     far = [ring_copy(two_back, c, nxt if c < 2 else prv, 8 + c) for c in range(4)]
 
+    def sort_group(group, carry):
+        for half in range(2):
+            table_copy(group, half).wait()
+            for two in range(4 * half, 4 * half + 4):
+                gather_two((table_a, table_b)[half], turned, held.at[two], two)
+                if two > 0:
+                    place_two(held.at[two - 1], rates, group, two - 1)
+                else:
+                    place_two(held.at[7], rates, jnp.maximum(group - 1, 0), 7)
+
+            @pl.when(group < GROUPS - 1)
+            def _():
+                table_copy(jnp.minimum(group + 1, GROUPS - 1), half).start()
+
+        return carry
+
     def relay(c):
         (from_prv if c < 2 else from_nxt)[c].wait_recv()
         relays[c].start()
+
+    lax.fori_loop(0, 4, sort_group, 0)
+    relay(0)
+    relay(2)
+    lax.fori_loop(4, 6, sort_group, 0)
+    relay(1)
+    relay(3)
+    lax.fori_loop(6, GROUPS, sort_group, 0)
+    place_two(held.at[7], rates, GROUPS - 1, 7)
+
+    own_copies[1].wait()
+    arrived(1)
+    arrived(2)
 
     def momenta(k, carry):
         rate = jnp.full((8, 128), speed[k], f32)
@@ -247,14 +267,7 @@
             out[d, k] = transported(own[d, k], before[d, k], after[d, k], rate)
         return carry
 
-    relay(0)
-    relay(2)
-    own_copies[1].wait()
-    arrived(1)
-    arrived(2)
     lax.fori_loop(0, LOCAL, momenta, 0)
-    relay(1)
-    relay(3)
 
     for c in range(2):
         from_prv[2 + c].wait_recv()
@@ -292,6 +305,8 @@
             for k in range(4):
                 source[pl.ds(k * 64 + 2 * c + half, 8, stride=8), :] = total[k * 8 : k * 8 + 8, half * 128 : half * 128 + 128]
 
+    for copy in late_copies:
+        copy.wait()
     row = lax.broadcasted_iota(i32, (8, 128), 0) & 3
     here_p = pres[...]
     above = jnp.where(row < 3, pltpu.roll(here_p, 7, 0), pltpu.roll(pres_after[...], 3, 0))
@@ -336,16 +351,25 @@
 
 
 def local(dust_state, drift_speed, stop_ratio, gas_rho, gas_vel, pressure, pair_list, outcome):
+    halo = pltpu.VMEM((4, LOCAL, 8, 128), f32)
+    cell = pltpu.VMEM((8, 128), f32)
     dma = pltpu.SemaphoreType.DMA
-    in_hbm = pl.BlockSpec(memory_space=pltpu.HBM)
-    in_vmem = pl.BlockSpec(memory_space=pltpu.VMEM)
-    in_smem = pl.BlockSpec(memory_space=pltpu.SMEM)
-    rates = pl.pallas_call(
-        sort_kernel,
-        out_shape=jax.ShapeDtypeStruct((BINS * 32, 128), bf16),
-        in_specs=[in_hbm, in_hbm],
-        out_specs=in_vmem,
+    result = pl.pallas_call(
+        step_kernel,
+        out_shape=jax.ShapeDtypeStruct((4, LOCAL, 8, 128), f32),
+        in_specs=[pl.BlockSpec(memory_space=pl.ANY)] * 8,
+        out_specs=pl.BlockSpec(memory_space=pltpu.VMEM),
         scratch_shapes=[
+            halo, halo, halo, cell, cell,
+            pltpu.VMEM((4 * 224, 128), f32),
+            pltpu.VMEM((160, 1024), bf16),
+            pltpu.VMEM((160, 1024), bf16),
+            pltpu.VMEM((256, 128), f32),
+            pltpu.SMEM((LOCAL,), f32),
+            pltpu.SMEM((LOCAL,), f32),
+            cell,
+            pltpu.VMEM((3, 8, 128), f32),
+            cell,
             pltpu.VMEM((2, PAIRS), i32),
             pltpu.VMEM((LOCAL, PAIRS), f32),
             pltpu.VMEM((PAIRS, 128), f32),
@@ -353,30 +377,17 @@
             pltpu.VMEM((BINS, 128), i32),
             pltpu.SMEM((8, 128), i32),
             pltpu.SMEM((8, 128), i32),
-            dma((2,)), dma((2,)),
-        ],
-        compiler_params=pltpu.CompilerParams(vmem_limit_bytes=24 << 20),
-        name="sort_rates",
-    )(pair_list.T, outcome.T)
-    halo = pltpu.VMEM((4, LOCAL, 8, 128), f32)
-    cell = pltpu.VMEM((8, 128), f32)
-    result = pl.pallas_call(
-        step_kernel,
-        out_shape=jax.ShapeDtypeStruct((4, LOCAL, 8, 128), f32),
-        in_specs=[pl.BlockSpec(memory_space=pl.ANY), in_smem, in_smem, in_vmem, in_vmem, in_vmem, in_vmem],
-        out_specs=in_vmem,
-        scratch_shapes=[
-            halo, halo, halo, cell, cell,
-            pltpu.VMEM((4 * 224, 128), f32),
-            pltpu.VMEM((160, 1024), bf16),
-            pltpu.VMEM((160, 1024), bf16),
-            pltpu.VMEM((256, 128), f32),
-            dma((2,)), dma((3,)), dma((3,)), dma((3,)), dma((3,)),
+            pltpu.VMEM((BINS * 32, 128), bf16),
+            dma((2,)), dma((7,)), dma((2,)),
+            dma((3,)), dma((3,)), dma((3,)), dma((3,)),
             dma((12,)), dma((12,)),
         ],
-        compiler_params=pltpu.CompilerParams(collective_id=0, has_side_effects=True, vmem_limit_bytes=24 << 20),
+        compiler_params=pltpu.CompilerParams(collective_id=0, has_side_effects=True),
         name="dust_step",
-    )(folded(dust_state), drift_speed, stop_ratio, folded(gas_rho), folded(gas_vel), folded(pressure), rates)
+    )(
+        folded(dust_state), drift_speed, stop_ratio, folded(gas_rho), folded(gas_vel), folded(pressure),
+        pair_list.T, outcome.T,
+    )
     return unfolded(result)
 
 

time: 45.7 us -> 36.8 us (0.81)
  Pallas kernels: 42.6 us -> 34.8 us
  local copies, waits for them, and re-layouts: 2.74 us -> 1.82 us
    pallas_call x1 -> x0, Pallas kernels: 8.7 us -> none  [local(): pl.pallas_call(sort_kernel, out_shape=jax.ShapeDtypeStruct((BINS * 32, 12...]
    unnamed x17 -> x1, local copies, waits for them, and re-layouts: 2.74 us -> 1.82 us
    pallas_call x1, Pallas kernels: 33.9 us -> 34.8 us  [local(): pl.pallas_call(step_kernel, out_shape=jax.ShapeDtypeStruct((4, LOCAL, 8,...]
where the time goes in v3:
time: 36.8 us; the launch traced here: 36.6 us
  Pallas kernels  34.8 us (95%)
  local copies, waits for them, and re-layouts  1.82 us (5%)
    pallas_call x1, Pallas kernels, local(): pl.pallas_call(step_kernel, out_shape=jax.ShapeDtypeStruct((4, LOCAL, 8,...  34.8 us
    unnamed x1, local copies, waits for them, and re-layouts  1.82 us

profile of v3, /device:TPU:6, one launch (start us, length us, event | category | flops | bytes accessed | tf_op | source)
XLA Modules:
  0.0 36.6 jit_solution(11875692332455132895)
XLA Ops:
  0.0 34.8 %dust_step.1 = f32[4,28,8,128]{3,2,1,0:T(8,128)} custom-call(f32[4,28,8,128]{3,2,1,0:T(8,128)} %bitcast.29, f32[28]{0:T(128)} %speed_in.1, f32[28]{0:T(128)} %stop_in.1, f32[8,128]{1,0:T(8,128)} %bitcast.32, f32[3,8,128]{2,1,0:T(8,128)} %bitcast.31, f32[8,128]{1,0:T(8,128)} %bitcast.33, s32[2,6328]{1,0:T(2,128)} %bitcast.30, f32[28,6328]{1,0:T(8,128)} %bitcast.28), custom_call_target="tpu_custom_call" | custom-call | tf_op jit(solution)/shard_map/dust_step/pallas_call | solution.py:357
  34.8 1.8 %copy.15 = f32[4,28,4,256]{3,2,1,0:T(4,128)} copy(f32[4,28,4,256]{3,2,1,0:T(4,128)} %bitcast.27) | data formatting | bytes 917504

commit v4 on v3

--- a/solution.py
+++ b/solution.py
@@ -11,6 +11,8 @@
 BINS = 112
 LOCAL = 28
 PAIRS = 6328
+HALF = BINS // 2
+UNITS = 7
 GROUPS = 7
 f32, bf16, i32 = jnp.float32, jnp.bfloat16, jnp.int32
 
@@ -43,18 +45,18 @@
     return row, slot
 
 
-def invert_pairs(pairs_ref, table_ref):
-    total = jnp.zeros((BINS, 128), f32)
+def invert_pairs(pairs_ref, table_ref, core):
+    total = jnp.zeros((HALF, 128), f32)
     for start in range(0, PAIRS, 256):
         width = min(256, PAIRS - start)
         row, slot = slots_of(pairs_ref[:, start : start + width])
-        rows = lax.broadcasted_iota(i32, (BINS, width), 0)
+        rows = lax.broadcasted_iota(i32, (HALF, width), 0)
         lanes = lax.broadcasted_iota(i32, (128, width), 0)
         number = start + 1 + lax.broadcasted_iota(i32, (1, width), 1)
         high = (number >> 6).astype(f32)
         low = (number & 63).astype(f32)
         value = jnp.where(lanes < 64, high, low)
-        first = jnp.where(rows == row, 1.0, 0.0).astype(bf16)
+        first = jnp.where(rows == row - HALF * core, 1.0, 0.0).astype(bf16)
         second = jnp.where((lanes & 63) == slot, value, 0.0).astype(bf16)
         total += lax.dot_general(first, second, (((1,), (1,)), ((), ())), preferred_element_type=f32)
     number = total * 64.0 + pltpu.roll(total, 64, 1)
@@ -72,18 +74,18 @@
         member = 2 * two + half
         for slot in range(member, 64):
             at = half * 64 + slot
-            index = table[member % 8, slot]
+            index = table[member, slot]
             held[at : at + 1, :] = turned[pl.ds(index, 1), :]
 
 
-def place_two(held, rates, group, two):
+def place_two(value, rates, unit, two):
     lane = lax.broadcasted_iota(i32, (32, 128), 1)
     left = lane < 64
-    unused = (lane < 2 * two) | ((lane >= 64) & (lane < 64 + 2 * two + 1))
-    value = jnp.where(unused, 0.0, held[...].T[0:32, :])
+    member = lax.rem(unit, 2) * 8 + 2 * two
+    value = jnp.where((lane & 63) < jnp.where(left, member, member + 1), 0.0, value)
     high = value.astype(bf16).astype(f32)
     low = pltpu.roll(value - high, 64, 1)
-    start = pl.multiple_of(group * 512 + two * 64, 64)
+    start = pl.multiple_of(unit * 256 + two * 64, 64)
     rates[pl.ds(start, 32), :] = jnp.where(left, high, low).astype(bf16)
     rates[pl.ds(start + 32, 32), :] = jnp.where(left, low, high).astype(bf16)
 
@@ -110,12 +112,13 @@
     dust_in, speed_in, stop_in, rho_in, vel_in, pres_in, pairs_in, outcome_in, out,
     own, before, after, pres_before, pres_after, dens, high, low, source,
     speed, stop, rho, vel, pres, pairs, outcome,
-    turned, held, table_v, table_a, table_b, rates,
-    own_sem, in_sem, table_sem, up_send, up_recv, down_send, down_recv, ring_send, ring_recv,
+    turned, held, turns, table_v, table_a, table_b, rates,
+    own_sem, in_sem, table_sem, up_send, up_recv, down_send, down_recv, ring_send, ring_recv, turn_send, turn_recv,
 ):
     tile, shard = lax.axis_index("tiles"), lax.axis_index("bins")
     tiles, shards = lax.axis_size("tiles"), lax.axis_size("bins")
     has_before, has_after = tile > 0, tile < tiles - 1
+    core = lax.rem(tile, 2)
     nxt, prv = lax.rem(shard + 1, shards), lax.rem(shard + shards - 1, shards)
 
     barrier = pltpu.get_barrier_semaphore()
@@ -188,14 +191,15 @@
             downs[part].wait_recv()
 
     pairs_copy.wait()
-    invert_pairs(pairs, table_v)
-
-    def table_copy(group, half):
-        rows = pl.ds(pl.multiple_of(group * 16 + half * 8, 8), 8)
-        return pltpu.make_async_copy(table_v.at[rows, :], (table_a, table_b)[half], table_sem.at[half])
-
-    table_copy(0, 0).start()
-    table_copy(0, 1).start()
+    invert_pairs(pairs, table_v, core)
+
+    tables = (table_a, table_b)
+
+    def table_copy(unit):
+        return pltpu.make_async_copy(table_v.at[8 * unit : 8 * unit + 8, :], tables[unit % 2], table_sem.at[unit % 2])
+
+    table_copy(0).start()
+    table_copy(1).start()
     outcome_copy.wait()
     turn_outcome(outcome, turned)
 
@@ -228,38 +232,56 @@
     relays = [ring_copy(prv, c, nxt, 8 + c) if c < 2 else ring_copy(nxt, c, prv, 8 + c) for c in range(4)]
     far = [ring_copy(two_back, c, nxt if c < 2 else prv, 8 + c) for c in range(4)]
 
-    def sort_group(group, carry):
-        for half in range(2):
-            table_copy(group, half).wait()
-            for two in range(4 * half, 4 * half + 4):
-                gather_two((table_a, table_b)[half], turned, held.at[two], two)
-                if two > 0:
-                    place_two(held.at[two - 1], rates, group, two - 1)
-                else:
-                    place_two(held.at[7], rates, jnp.maximum(group - 1, 0), 7)
-
-            @pl.when(group < GROUPS - 1)
-            def _():
-                table_copy(jnp.minimum(group + 1, GROUPS - 1), half).start()
-
-        return carry
+    first_unit = core * UNITS
+    other_unit = UNITS - first_unit
+
+    def turn_copy(unit):
+        piece = turns.at[pl.ds((first_unit + unit) * 4, 4)]
+        return pltpu.make_async_remote_copy(
+            piece, piece, turn_send.at[unit], turn_recv.at[unit],
+            device_id={"tiles": tile + 1 - 2 * core}, device_id_type=MESH,
+        )
+
+    def arriving(unit):
+        piece = turns.at[pl.ds((other_unit + unit) * 4, 4)]
+        return pltpu.make_async_remote_copy(
+            piece, piece, turn_send.at[unit], turn_recv.at[unit],
+            device_id={"tiles": tile + 1 - 2 * core}, device_id_type=MESH,
+        )
+
+    def finish(unit, two):
+        value = held[(unit % 2) * 4 + two].T[0:32, :]
+        turns[(first_unit + unit) * 4 + two] = value
+        place_two(value, rates, first_unit + unit, two)
+
+    def sort_unit(unit):
+        table_copy(unit).wait()
+        for two in range(4):
+            gather_two(tables[unit % 2], turned, held.at[(unit % 2) * 4 + two], two)
+            if two > 0:
+                finish(unit, two - 1)
+            elif unit > 0:
+                finish(unit - 1, 3)
+        if unit > 0:
+            turn_copy(unit - 1).start()
+        if unit + 2 < UNITS:
+            table_copy(unit + 2).start()
 
     def relay(c):
         (from_prv if c < 2 else from_nxt)[c].wait_recv()
         relays[c].start()
 
-    lax.fori_loop(0, 4, sort_group, 0)
+    for unit in range(6):
+        sort_unit(unit)
     relay(0)
     relay(2)
-    lax.fori_loop(4, 6, sort_group, 0)
-    relay(1)
-    relay(3)
-    lax.fori_loop(6, GROUPS, sort_group, 0)
-    place_two(held.at[7], rates, GROUPS - 1, 7)
+    sort_unit(6)
+    finish(6, 3)
 
     own_copies[1].wait()
     arrived(1)
     arrived(2)
+    turn_copy(6).start()
 
     def momenta(k, carry):
         rate = jnp.full((8, 128), speed[k], f32)
@@ -268,6 +290,18 @@
         return carry
 
     lax.fori_loop(0, LOCAL, momenta, 0)
+    relay(1)
+    relay(3)
+
+    for unit in range(UNITS):
+        arriving(unit).wait_recv()
+
+    def place_unit(unit, carry):
+        for two in range(4):
+            place_two(turns[(other_unit + unit) * 4 + two], rates, other_unit + unit, two)
+        return carry
+
+    lax.fori_loop(0, UNITS, place_unit, 0)
 
     for c in range(2):
         from_prv[2 + c].wait_recv()
@@ -326,7 +360,7 @@
             grown = out[d + 1, k] + half * gas[d]
             out[d + 1, k] = (grown + pull * target[d]) * share
 
-    for copy in (*sends, *relays):
+    for copy in (*sends, *relays, *[turn_copy(unit) for unit in range(UNITS)]):
         copy.wait_send()
     for part in range(3):
         @pl.when(has_after)
@@ -374,13 +408,14 @@
             pltpu.VMEM((LOCAL, PAIRS), f32),
             pltpu.VMEM((PAIRS, 128), f32),
             pltpu.VMEM((8, 128, 128), f32),
-            pltpu.VMEM((BINS, 128), i32),
+            pltpu.VMEM((2 * UNITS * 4, 32, 128), f32),
+            pltpu.VMEM((HALF, 128), i32),
             pltpu.SMEM((8, 128), i32),
             pltpu.SMEM((8, 128), i32),
             pltpu.VMEM((BINS * 32, 128), bf16),
             dma((2,)), dma((7,)), dma((2,)),
             dma((3,)), dma((3,)), dma((3,)), dma((3,)),
-            dma((12,)), dma((12,)),
+            dma((12,)), dma((12,)), dma((UNITS,)), dma((UNITS,)),
         ],
         compiler_params=pltpu.CompilerParams(collective_id=0, has_side_effects=True),
         name="dust_step",

time: 36.8 us -> 36.9 us (level)
  no operation moved by 1% of the time
where the time goes in v4:
time: 36.9 us; the launch traced here: 36.7 us
  Pallas kernels  34.9 us (95%)
  local copies, waits for them, and re-layouts  1.82 us (5%)
    pallas_call x1, Pallas kernels, local(): pl.pallas_call(step_kernel, out_shape=jax.ShapeDtypeStruct((4, LOCAL, 8,...  34.9 us
    unnamed x1, local copies, waits for them, and re-layouts  1.82 us

profile of v4, /device:TPU:6, one launch (start us, length us, event | category | flops | bytes accessed | tf_op | source)
XLA Modules:
  0.0 36.7 jit_solution(8546268710512666578)
XLA Ops:
  0.0 34.9 %dust_step.1 = f32[4,28,8,128]{3,2,1,0:T(8,128)} custom-call(f32[4,28,8,128]{3,2,1,0:T(8,128)} %bitcast.29, f32[28]{0:T(128)} %speed_in.1, f32[28]{0:T(128)} %stop_in.1, f32[8,128]{1,0:T(8,128)} %bitcast.32, f32[3,8,128]{2,1,0:T(8,128)} %bitcast.31, f32[8,128]{1,0:T(8,128)} %bitcast.33, s32[2,6328]{1,0:T(2,128)} %bitcast.30, f32[28,6328]{1,0:T(8,128)} %bitcast.28), custom_call_target="tpu_custom_call" | custom-call | tf_op jit(solution)/shard_map/dust_step/pallas_call | solution.py:391
  34.9 1.8 %copy.15 = f32[4,28,4,256]{3,2,1,0:T(4,128)} copy(f32[4,28,4,256]{3,2,1,0:T(4,128)} %bitcast.27) | data formatting | bytes 917504

commit v5 on v4

--- a/solution.py
+++ b/solution.py
@@ -390,7 +390,7 @@
     dma = pltpu.SemaphoreType.DMA
     result = pl.pallas_call(
         step_kernel,
-        out_shape=jax.ShapeDtypeStruct((4, LOCAL, 8, 128), f32),
+        out_shape=pltpu.VMEM((4, LOCAL, 8, 128), f32),
         in_specs=[pl.BlockSpec(memory_space=pl.ANY)] * 8,
         out_specs=pl.BlockSpec(memory_space=pltpu.VMEM),
         scratch_shapes=[

time: 36.9 us -> 35 us (0.949)
  local copies, waits for them, and re-layouts: 1.82 us -> 0.77 us
  Pallas kernels: 34.9 us -> 34.1 us
    unnamed x1, local copies, waits for them, and re-layouts: 1.82 us -> 0.77 us
    pallas_call x1, Pallas kernels: 34.9 us -> 34.1 us  [local(): pl.pallas_call(step_kernel, out_shape=pltpu.VMEM((4, LOCAL, 8, 128), f32)...]
where the time goes in v5:
time: 35 us; the launch traced here: 34.9 us
  Pallas kernels  34.1 us (97%)
  local copies, waits for them, and re-layouts  0.77 us (2%)
    pallas_call x1, Pallas kernels, local(): pl.pallas_call(step_kernel, out_shape=pltpu.VMEM((4, LOCAL, 8, 128), f32)...  34.1 us
    unnamed x1, local copies, waits for them, and re-layouts  0.77 us

profile of v5, /device:TPU:6, one launch (start us, length us, event | category | flops | bytes accessed | tf_op | source)
XLA Modules:
  0.0 34.9 jit_solution(12463289615393161780)
XLA Ops:
  0.0 34.1 %dust_step.1 = f32[4,28,8,128]{3,2,1,0:T(8,128)S(1)} custom-call(f32[4,28,8,128]{3,2,1,0:T(8,128)} %bitcast.29, f32[28]{0:T(128)} %speed_in.1, f32[28]{0:T(128)} %stop_in.1, f32[8,128]{1,0:T(8,128)} %bitcast.32, f32[3,8,128]{2,1,0:T(8,128)} %bitcast.31, f32[8,128]{1,0:T(8,128)} %bitcast.33, s32[2,6328]{1,0:T(2,128)} %bitcast.30, f32[28,6328]{1,0:T(8,128)} %bitcast.28), custom_call_target="tpu_custom_call" | custom-call | tf_op jit(solution)/shard_map/dust_step/pallas_call | solution.py:391
  34.1 0.8 %copy.15 = f32[4,28,4,256]{3,2,1,0:T(4,128)} copy(f32[4,28,4,256]{3,2,1,0:T(4,128)S(1)} %bitcast.27) | data formatting | bytes 917504

commit v6 on v5

--- a/solution.py
+++ b/solution.py
@@ -18,38 +18,46 @@
 
 
 def bin_at(group, member):
-    if group < 6:
-        tile = 2 * group + member // 8
-        return tile // 3, (tile % 3) * 8 + member % 8
-    return member // 4, 24 + member % 4
-
-
-def group_member(index):
-    shard = (index >= 28).astype(i32) + (index >= 56).astype(i32) + (index >= 84).astype(i32)
-    own = index - 28 * shard
-    tile = 3 * shard + (own >> 3)
-    full = own < 24
-    group = jnp.where(full, tile >> 1, 6)
-    member = jnp.where(full, ((tile & 1) << 3) + (own & 7), 4 * shard + own - 24)
-    return group, member
-
-
-def slots_of(pairs):
-    group_i, member_i = group_member(pairs[0:1, :])
-    group_j, member_j = group_member(pairs[1:2, :])
+    tile, low = 2 * group + member // 8, member % 8
+    if tile < 9:
+        return tile // 3, (tile % 3) * 8 + low
+    if tile == 9:
+        return low // 4, 24 + low % 4
+    if tile < 13:
+        return 3, (tile - 10) * 8 + low
+    return 2 + low // 4, 24 + low % 4
+
+
+def group_member(index, shard):
+    owner = (index >= 28).astype(i32) + (index >= 56).astype(i32) + (index >= 84).astype(i32)
+    own = index - 28 * owner
+    ahead = (owner - shard) & 3
+    block = jnp.where(ahead == 2, 3, jnp.where(ahead == 3, 2, ahead))
+    full = jnp.where(block == 3, 10, 3 * block) + (own >> 3)
+    left = jnp.where(block < 2, 9, 13)
+    is_full = own < 24
+    tile = jnp.where(is_full, full, left)
+    low = jnp.where(is_full, own & 7, ((block & 1) << 2) + own - 24)
+    return tile >> 1, ((tile & 1) << 3) + low
+
+
+def slots_of(pairs, shard):
+    group_i, member_i = group_member(pairs[0:1, :], shard)
+    group_j, member_j = group_member(pairs[1:2, :], shard)
     ahead = group_j - group_i
     ahead = jnp.where(ahead < 0, ahead + GROUPS, ahead)
-    keep = ahead <= 3
+    keep = (ahead <= 3) & ((ahead > 0) | (member_i <= member_j))
+    ahead = jnp.where((ahead == 0) & ~keep, GROUPS, ahead)
     row = jnp.where(keep, group_i * 16 + member_i, group_j * 16 + member_j)
     slot = jnp.where(keep, ahead * 16 + member_j, (GROUPS - ahead) * 16 + member_i)
     return row, slot
 
 
-def invert_pairs(pairs_ref, table_ref, core):
+def invert_pairs(pairs_ref, table_ref, core, shard):
     total = jnp.zeros((HALF, 128), f32)
     for start in range(0, PAIRS, 256):
         width = min(256, PAIRS - start)
-        row, slot = slots_of(pairs_ref[:, start : start + width])
+        row, slot = slots_of(pairs_ref[:, start : start + width], shard)
         rows = lax.broadcasted_iota(i32, (HALF, width), 0)
         lanes = lax.broadcasted_iota(i32, (128, width), 0)
         number = start + 1 + lax.broadcasted_iota(i32, (1, width), 1)
@@ -110,7 +118,7 @@
 
 def step_kernel(
     dust_in, speed_in, stop_in, rho_in, vel_in, pres_in, pairs_in, outcome_in, out,
-    own, before, after, pres_before, pres_after, dens, high, low, source,
+    own, before, after, pres_before, pres_after, dens, high, low, partial, source,
     speed, stop, rho, vel, pres, pairs, outcome,
     turned, held, turns, table_v, table_a, table_b, rates,
     own_sem, in_sem, table_sem, up_send, up_recv, down_send, down_recv, ring_send, ring_recv, turn_send, turn_recv,
@@ -191,7 +199,7 @@
             downs[part].wait_recv()
 
     pairs_copy.wait()
-    invert_pairs(pairs, table_v, core)
+    invert_pairs(pairs, table_v, core, shard)
 
     tables = (table_a, table_b)
 
@@ -206,31 +214,27 @@
     own_copies[0].wait()
     speed_copy.wait()
     arrived(0)
-    here = shard * 224
     for k in range(LOCAL):
         moved = transported(own[0, k], before[0, k], after[0, k], jnp.full((8, 128), speed[k], f32))
         out[0, k] = moved
-        dens[pl.ds(here + k, 8, stride=LOCAL), :] = moved
-
-    def ring_copy(block, chunk, target, slot):
-        piece = dens.at[pl.ds(pl.multiple_of(block * 224 + chunk * 56, 8), 56), :]
+        dens[pl.ds(k, 8, stride=LOCAL), :] = moved
+
+    def ring_copy(block, there, chunk, target, slot):
+        make = lambda at: dens.at[at * 224 + chunk * 56 : at * 224 + chunk * 56 + 56, :]
         return pltpu.make_async_remote_copy(
-            piece, piece, ring_send.at[slot], ring_recv.at[slot],
+            make(block), make(there), ring_send.at[slot], ring_recv.at[slot],
             device_id={"bins": target}, device_id_type=MESH,
         )
 
-    two_back = lax.rem(shard + 2, shards)
     forward, backward, relayed = (0, 1, 2, 3), (2, 3, 0, 1), (0, 2, 1, 3)
+    to_nxt = [ring_copy(0, 2, c, nxt, c) for c in range(4)]
+    to_prv = [ring_copy(0, 1, c, prv, 4 + c) for c in range(4)]
+    relays = [ring_copy(2, 3, c, nxt, 8 + c) if c < 2 else ring_copy(1, 3, c, prv, 8 + c) for c in range(4)]
     sends = []
     for i in range(4):
-        sends.append(ring_copy(shard, forward[i], nxt, forward[i]))
-        sends.append(ring_copy(shard, backward[i], prv, 4 + backward[i]))
+        sends += [to_nxt[forward[i]], to_prv[backward[i]]]
     for copy in sends:
         copy.start()
-    from_prv = [ring_copy(prv, c, nxt, c) for c in range(4)]
-    from_nxt = [ring_copy(nxt, c, prv, 4 + c) for c in range(4)]
-    relays = [ring_copy(prv, c, nxt, 8 + c) if c < 2 else ring_copy(nxt, c, prv, 8 + c) for c in range(4)]
-    far = [ring_copy(two_back, c, nxt if c < 2 else prv, 8 + c) for c in range(4)]
 
     first_unit = core * UNITS
     other_unit = UNITS - first_unit
@@ -268,7 +272,7 @@
             table_copy(unit + 2).start()
 
     def relay(c):
-        (from_prv if c < 2 else from_nxt)[c].wait_recv()
+        (to_nxt if c < 2 else to_prv)[c].wait_recv()
         relays[c].start()
 
     for unit in range(6):
@@ -304,18 +308,19 @@
     lax.fori_loop(0, UNITS, place_unit, 0)
 
     for c in range(2):
-        from_prv[2 + c].wait_recv()
-        from_nxt[c].wait_recv()
-
-    for c in relayed:
-        far[c].wait_recv()
+        to_nxt[2 + c].wait_recv()
+        to_prv[c].wait_recv()
+
+    def split(c, groups):
         for m in (2 * c, 2 * c + 1):
-            for group in range(GROUPS):
-                if group < 6:
-                    starts = [bin_at(group, 0), bin_at(group, 8)]
-                    pieces = [dens[b * 224 + m * 28 + w : b * 224 + m * 28 + w + 8, :] for b, w in starts]
-                else:
-                    pieces = [dens[b * 224 + m * 28 + 24 : b * 224 + m * 28 + 28, :] for b in range(4)]
+            for group in groups:
+                pieces, member = [], 0
+                while member < 16:
+                    b, w = bin_at(group, member)
+                    size = 8 if w < 24 else 4
+                    start = b * 224 + m * 28 + w
+                    pieces.append(dens[start : start + size, :])
+                    member += size
                 value = jnp.concatenate(pieces, 0)
                 top = value.astype(bf16)
                 rest = (value - top.astype(f32)).astype(bf16)
@@ -323,8 +328,9 @@
                     if at < 10:
                         high[at * 16 : at * 16 + 16, m * 128 : m * 128 + 128] = top
                         low[at * 16 : at * 16 + 16, m * 128 : m * 128 + 128] = rest
-        total = jnp.zeros((32, 256), f32)
-        for group in range(GROUPS):
+
+    def multiply(c, groups, total):
+        for group in groups:
             top = high[group * 16 : group * 16 + 64, c * 256 : c * 256 + 256]
             rest = low[group * 16 : group * 16 + 64, c * 256 : c * 256 + 256]
             weights = jnp.concatenate([top, top, rest, rest], 0)
@@ -335,6 +341,16 @@
                 start = b * 224 + w + c * 56
                 line = jnp.concatenate([dens[start : start + 1, :], dens[start + 28 : start + 29, :]], 1)
                 total += product[member * 32 : member * 32 + 32, :] * line
+        return total
+
+    for c in relayed:
+        split(c, range(5))
+        partial[c] = multiply(c, range(2), jnp.zeros((32, 256), f32))
+
+    for c in relayed:
+        relays[c].wait_recv()
+        split(c, range(5, GROUPS))
+        total = multiply(c, range(2, GROUPS), partial[c])
         for half in range(2):
             for k in range(4):
                 source[pl.ds(k * 64 + 2 * c + half, 8, stride=8), :] = total[k * 8 : k * 8 + 8, half * 128 : half * 128 + 128]
@@ -398,6 +414,7 @@
             pltpu.VMEM((4 * 224, 128), f32),
             pltpu.VMEM((160, 1024), bf16),
             pltpu.VMEM((160, 1024), bf16),
+            pltpu.VMEM((4, 32, 256), f32),
             pltpu.VMEM((256, 128), f32),
             pltpu.SMEM((LOCAL,), f32),
             pltpu.SMEM((LOCAL,), f32),

time: 35 us -> 34.1 us (0.974)
  Pallas kernels: 34.1 us -> 33.2 us
    pallas_call x1, Pallas kernels: 34.1 us -> 33.2 us  [local(): pl.pallas_call(step_kernel, out_shape=pltpu.VMEM((4, LOCAL, 8, 128), f32)...]
where the time goes in v6:
time: 34.1 us; the launch traced here: 33.9 us
  Pallas kernels  33.2 us (97%)
  local copies, waits for them, and re-layouts  0.77 us (2%)
    pallas_call x1, Pallas kernels, local(): pl.pallas_call(step_kernel, out_shape=pltpu.VMEM((4, LOCAL, 8, 128), f32)...  33.2 us
    unnamed x1, local copies, waits for them, and re-layouts  0.77 us

profile of v6, /device:TPU:6, one launch (start us, length us, event | category | flops | bytes accessed | tf_op | source)
XLA Modules:
  0.0 33.9 jit_solution(12309910606131470973)
XLA Ops:
  0.0 33.2 %dust_step.1 = f32[4,28,8,128]{3,2,1,0:T(8,128)S(1)} custom-call(f32[4,28,8,128]{3,2,1,0:T(8,128)} %bitcast.29, f32[28]{0:T(128)} %speed_in.1, f32[28]{0:T(128)} %stop_in.1, f32[8,128]{1,0:T(8,128)} %bitcast.32, f32[3,8,128]{2,1,0:T(8,128)} %bitcast.31, f32[8,128]{1,0:T(8,128)} %bitcast.33, s32[2,6328]{1,0:T(2,128)} %bitcast.30, f32[28,6328]{1,0:T(8,128)} %bitcast.28), custom_call_target="tpu_custom_call" | custom-call | tf_op jit(solution)/shard_map/dust_step/pallas_call | solution.py:407
  33.2 0.8 %copy.15 = f32[4,28,4,256]{3,2,1,0:T(4,128)} copy(f32[4,28,4,256]{3,2,1,0:T(4,128)S(1)} %bitcast.27) | data formatting | bytes 917504

commit v7 on v6

--- a/solution.py
+++ b/solution.py
@@ -275,17 +275,31 @@
         (to_nxt if c < 2 else to_prv)[c].wait_recv()
         relays[c].start()
 
+    def place_units(first, last):
+        for unit in range(first, last):
+            arriving(unit).wait_recv()
+
+        def place_unit(unit, carry):
+            for two in range(4):
+                place_two(turns[(other_unit + unit) * 4 + two], rates, other_unit + unit, two)
+            return carry
+
+        lax.fori_loop(first, last, place_unit, 0)
+
     for unit in range(6):
         sort_unit(unit)
     relay(0)
     relay(2)
     sort_unit(6)
     finish(6, 3)
+    place_units(0, 5)
+    turn_copy(6).start()
+    relay(1)
+    relay(3)
 
     own_copies[1].wait()
     arrived(1)
     arrived(2)
-    turn_copy(6).start()
 
     def momenta(k, carry):
         rate = jnp.full((8, 128), speed[k], f32)
@@ -294,18 +308,7 @@
         return carry
 
     lax.fori_loop(0, LOCAL, momenta, 0)
-    relay(1)
-    relay(3)
-
-    for unit in range(UNITS):
-        arriving(unit).wait_recv()
-
-    def place_unit(unit, carry):
-        for two in range(4):
-            place_two(turns[(other_unit + unit) * 4 + two], rates, other_unit + unit, two)
-        return carry
-
-    lax.fori_loop(0, UNITS, place_unit, 0)
+    place_units(5, UNITS)
 
     for c in range(2):
         to_nxt[2 + c].wait_recv()

time: 34.1 us -> 33.9 us (level)
  no operation moved by 1% of the time
where the time goes in v7:
time: 33.9 us; the launch traced here: 33.7 us
  Pallas kernels  32.9 us (97%)
  local copies, waits for them, and re-layouts  0.77 us (2%)
    pallas_call x1, Pallas kernels, local(): pl.pallas_call(step_kernel, out_shape=pltpu.VMEM((4, LOCAL, 8, 128), f32)...  32.9 us
    unnamed x1, local copies, waits for them, and re-layouts  0.77 us

profile of v7, /device:TPU:6, one launch (start us, length us, event | category | flops | bytes accessed | tf_op | source)
XLA Modules:
  0.0 33.7 jit_solution(6092904044376284270)
XLA Ops:
  0.0 32.9 %dust_step.1 = f32[4,28,8,128]{3,2,1,0:T(8,128)S(1)} custom-call(f32[4,28,8,128]{3,2,1,0:T(8,128)} %bitcast.29, f32[28]{0:T(128)} %speed_in.1, f32[28]{0:T(128)} %stop_in.1, f32[8,128]{1,0:T(8,128)} %bitcast.32, f32[3,8,128]{2,1,0:T(8,128)} %bitcast.31, f32[8,128]{1,0:T(8,128)} %bitcast.33, s32[2,6328]{1,0:T(2,128)} %bitcast.30, f32[28,6328]{1,0:T(8,128)} %bitcast.28), custom_call_target="tpu_custom_call" | custom-call | tf_op jit(solution)/shard_map/dust_step/pallas_call | solution.py:410
  32.9 0.8 %copy.15 = f32[4,28,4,256]{3,2,1,0:T(4,128)} copy(f32[4,28,4,256]{3,2,1,0:T(4,128)S(1)} %bitcast.27) | data formatting | bytes 917504

commit v8 on v7

--- a/solution.py
+++ b/solution.py
@@ -110,9 +110,10 @@
     row = lax.broadcasted_iota(i32, (8, 128), 0) & 3
     result = (1.0 - 1.5 * a + 1.125 * (a * a)) * own
     up, down = weights(forward), weights(backward)
+    before_swap, after_swap = pltpu.roll(before, 4, 0), pltpu.roll(after, 4, 0)
     for m in (1, 2, 3):
-        result += up[m - 1] * jnp.where(row >= m, pltpu.roll(own, m, 0), pltpu.roll(before, 4 + m, 0))
-        result += down[m - 1] * jnp.where(row < 4 - m, pltpu.roll(own, 8 - m, 0), pltpu.roll(after, 4 - m, 0))
+        result += up[m - 1] * pltpu.roll(jnp.where(row < 4 - m, own, before_swap), m, 0)
+        result += down[m - 1] * pltpu.roll(jnp.where(row >= m, own, after_swap), 8 - m, 0)
     return result + up[3] * before + down[3] * after
 
 
@@ -233,7 +234,7 @@
     sends = []
     for i in range(4):
         sends += [to_nxt[forward[i]], to_prv[backward[i]]]
-    for copy in sends:
+    for copy in sends[0:4]:
         copy.start()
 
     first_unit = core * UNITS
@@ -288,8 +289,13 @@
 
     for unit in range(6):
         sort_unit(unit)
+        if unit == 1:
+            sends[4].start()
+            sends[5].start()
     relay(0)
     relay(2)
+    sends[6].start()
+    sends[7].start()
     sort_unit(6)
     finish(6, 3)
     place_units(0, 5)

time: 33.9 us -> 35.5 us (1.047)
  Pallas kernels: 32.9 us -> 34.6 us
    pallas_call x1, Pallas kernels: 32.9 us -> 34.6 us  [local(): pl.pallas_call(step_kernel, out_shape=pltpu.VMEM((4, LOCAL, 8, 128), f32)...]
where the time goes in v8:
time: 35.5 us; the launch traced here: 35.4 us
  Pallas kernels  34.6 us (97%)
  local copies, waits for them, and re-layouts  0.77 us (2%)
    pallas_call x1, Pallas kernels, local(): pl.pallas_call(step_kernel, out_shape=pltpu.VMEM((4, LOCAL, 8, 128), f32)...  34.6 us
    unnamed x1, local copies, waits for them, and re-layouts  0.77 us

profile of v8, /device:TPU:6, one launch (start us, length us, event | category | flops | bytes accessed | tf_op | source)
XLA Modules:
  0.0 35.4 jit_solution(16500549576030527833)
XLA Ops:
  0.0 34.6 %dust_step.1 = f32[4,28,8,128]{3,2,1,0:T(8,128)S(1)} custom-call(f32[4,28,8,128]{3,2,1,0:T(8,128)} %bitcast.29, f32[28]{0:T(128)} %speed_in.1, f32[28]{0:T(128)} %stop_in.1, f32[8,128]{1,0:T(8,128)} %bitcast.32, f32[3,8,128]{2,1,0:T(8,128)} %bitcast.31, f32[8,128]{1,0:T(8,128)} %bitcast.33, s32[2,6328]{1,0:T(2,128)} %bitcast.30, f32[28,6328]{1,0:T(8,128)} %bitcast.28), custom_call_target="tpu_custom_call" | custom-call | tf_op jit(solution)/shard_map/dust_step/pallas_call | solution.py:416
  34.6 0.8 %copy.15 = f32[4,28,4,256]{3,2,1,0:T(4,128)} copy(f32[4,28,4,256]{3,2,1,0:T(4,128)S(1)} %bitcast.27) | data formatting | bytes 917504
